TPU v7x, 256 devices: a whole 4x4x8 slice. The times are simulated.
256 devices in a mesh: grp: 4 (over z_hi), gx: 16 (over z_lo, y, core), gy: 4 (over x).
Axes of the slice: x: 4, y: 4, z: 8 (z_hi: 4, z_lo: 2; z = z_hi * 2 + z_lo), core: 2. Of those that a mesh axis runs over, the one named last changes fastest.
Arguments:
- populations: float32 [27, 64, 32, 512], P(None, 'gx', 'gy', 'grp'), may hold values from 0 to 1, as said below
- thermal: float32 [7, 64, 32, 512], P(None, ('gx', 'grp'), 'gy'), may hold values from 0 to 1, as said below
- velocity_prev: float32 [3, 64, 32, 512], P(None, 'gx', 'gy', 'grp'), may hold values from -0.3 to 0.3
- solid: int32 [64, 32, 512], P('gx', 'gy', 'grp'), may hold values 0 or 1
- phase_ids: int32 [64, 32, 512], P(('gx', 'grp'), 'gy'), may hold values from 0 to 3
- conductivity: float32 [4], replicated, may hold values from 0.02 to 0.3
- rates: float32 [27], replicated, may hold values from 0.7 to 1.7
Outputs:
- populations_out: float32 [27, 64, 32, 512], P(None, 'gx', 'gy', 'grp')
- thermal_out: float32 [7, 64, 32, 512], P(None, ('gx', 'grp'), 'gy')
Inputs may be any that keep to these rules, and one draw needn't show every extreme that they name: `populations`: positive. `thermal`: positive.
All inputs are finite; a program needn't handle non-finite values. No bound on the sum of `solid` on one device may be relied on, other than what follows from the above.
Results may differ from a plain program's by a relative error of at most 0.0001.
Values sent between devices are 32-bit elements; how exact they have to be, the bound alone decides.
A program may use at most 64 MiB of HBM per device.

v0:
```python
import jax
import jax.numpy as jnp
import numpy as np
from jax import lax
from jax.sharding import PartitionSpec as P

STEPS = 4
WINDOWS = 2


HIGHEST = lax.Precision.HIGHEST
BUOYANCY = 0.03
REFERENCE_HEAT = 1.0
OFFSET_TABLE = [(number // 9 - 1, number // 3 % 3 - 1, number % 3 - 1) for number in range(27)]
LATTICE_WEIGHTS = np.array(
    [
        np.prod([2.0 / 3.0 if component == 0 else 1.0 / 6.0 for component in triple])
        for triple in OFFSET_TABLE
    ]
)
VANDERMONDE = np.array([[1.0, 1.0, 1.0], [-1.0, 0.0, 1.0], [1.0, 0.0, 1.0]])
VANDER_INVERSE = np.array([[0.0, -0.5, 0.5], [1.0, 0.0, -1.0], [0.0, 0.5, 0.5]])
MOMENT_MATRIX = np.kron(np.kron(VANDERMONDE, VANDERMONDE), VANDERMONDE)
MOMENT_INVERSE = np.kron(np.kron(VANDER_INVERSE, VANDER_INVERSE), VANDER_INVERSE)
RELAXED = np.array([0.0 if number in (0, 1, 3, 9) else 1.0 for number in range(27)])
SUMMING = np.concatenate([np.ones((1, 27)), 1.0 * np.array(OFFSET_TABLE).T], axis=0)
HEAT_WEIGHTS = np.array([0.25] + [0.125] * 6)


def from_behind(value, axis, steps):
    count = lax.axis_size(axis)
    pairs = [(source, (source + steps) % count) for source in range(count)]
    return lax.ppermute(value, axis, pairs)


def extended(cells, sides, width):
    for axis, dim in sides:
        count = lax.axis_size(axis)
        head = lax.slice_in_dim(cells, 0, width, axis=dim)
        tail = lax.slice_in_dim(cells, cells.shape[dim] - width, cells.shape[dim], axis=dim)
        cells = jnp.concatenate(
            [
                lax.ppermute(tail, axis, [(i, (i + 1) % count) for i in range(count)]),
                cells,
                lax.ppermute(head, axis, [((i + 1) % count, i) for i in range(count)]),
            ],
            axis=dim,
        )
    return cells


def flow_state(flat, heat_flat):
    sums = jnp.dot(jnp.asarray(SUMMING, jnp.float32), flat, precision=HIGHEST)
    density = sums[0]
    force = BUOYANCY * (heat_flat - REFERENCE_HEAT)
    speed = jnp.stack([sums[1], sums[2], sums[3] + 0.5 * force]) / density
    return (density, force, speed)


def collide(popul, heat, rates):
    flat = popul.reshape(27, -1)
    density, force, speed = flow_state(flat, heat.reshape(-1))
    along = jnp.dot(jnp.asarray(SUMMING[1:].T, jnp.float32), speed, precision=HIGHEST)
    square = jnp.sum(speed * speed, axis=0)
    balance = (
        density
        * jnp.asarray(LATTICE_WEIGHTS, jnp.float32)[:, None]
        * (1.0 + 3.0 * along + 4.5 * along * along - 1.5 * square)
    )
    scaled = (
        jnp.asarray(MOMENT_INVERSE, jnp.float32)
        * (rates * jnp.asarray(RELAXED, jnp.float32))[None, :]
    )
    relax = jnp.dot(scaled, jnp.asarray(MOMENT_MATRIX, jnp.float32), precision=HIGHEST)
    post = (
        flat
        - jnp.dot(relax, flat - balance, precision=HIGHEST)
        + jnp.asarray(MOMENT_INVERSE[:, 1], jnp.float32)[:, None] * force[None, :]
    )
    return post.reshape(popul.shape)


def flow_speed(popul, heat, solid):
    density, force, speed = flow_state(popul.reshape(27, -1), heat.reshape(-1))
    return jnp.where(solid[None] == 0, speed.reshape((3,) + solid.shape), 0.0)


def heat_collide(heat_pops, speed, relax_time):
    total = jnp.sum(heat_pops, axis=0)
    still = jnp.zeros_like(speed[0])
    along = jnp.stack([still, speed[0], -speed[0], speed[1], -speed[1], speed[2], -speed[2]])
    balance = (
        jnp.asarray(HEAT_WEIGHTS, jnp.float32)[:, None, None, None]
        * total[None]
        * (1.0 + 4.0 * along)
    )
    return heat_pops - (heat_pops - balance) / relax_time[None]


def relaxation(phase_ids, conductivity):
    levels = jnp.arange(conductivity.shape[0], dtype=jnp.int32)
    chosen = jnp.sum(
        jnp.where(
            phase_ids[None] == levels[:, None, None, None], conductivity[:, None, None, None], 0.0
        ),
        axis=0,
    )
    return 0.5 + 4.0 * chosen


def inner_window(padded, triple, sizes):
    return padded[
        1 - triple[0] : 1 - triple[0] + sizes[0],
        1 - triple[1] : 1 - triple[1] + sizes[1],
        1 - triple[2] : 1 - triple[2] + sizes[2],
    ]


def advance(grid, axis_number, send_up, send_down):
    space = 3 + axis_number
    length = grid.shape[space]
    rising = lax.index_in_dim(grid, 2, axis_number, keepdims=True)
    resting = lax.index_in_dim(grid, 1, axis_number, keepdims=True)
    falling = lax.index_in_dim(grid, 0, axis_number, keepdims=True)
    from_below = send_up(lax.slice_in_dim(rising, length - 1, length, axis=space))
    from_above = send_down(lax.slice_in_dim(falling, 0, 1, axis=space))
    rising = jnp.concatenate(
        [from_below, lax.slice_in_dim(rising, 0, length - 1, axis=space)], axis=space
    )
    falling = jnp.concatenate(
        [lax.slice_in_dim(falling, 1, length, axis=space), from_above], axis=space
    )
    return jnp.concatenate([falling, resting, rising], axis=axis_number)


def flow_arrivals(post):
    sizes = post.shape[1:]
    grid = post.reshape((3, 3, 3) + sizes)
    grid = advance(
        grid,
        0,
        lambda plane: from_behind(plane, "gx", 1),
        lambda plane: from_behind(plane, "gx", -1),
    )
    grid = advance(
        grid,
        1,
        lambda plane: from_behind(plane, "gy", 1),
        lambda plane: from_behind(plane, "gy", -1),
    )
    grid = advance(
        grid,
        2,
        lambda plane: from_behind(plane, "grp", 1),
        lambda plane: from_behind(plane, "grp", -1),
    )
    return grid.reshape(post.shape)


def stream_heat(post, grp_index, last_grp):
    length = post.shape[1]
    size_y = post.shape[2]
    eastward = post[1]
    westward = post[2]
    lower_first = from_behind(eastward, "grp", 1)
    lower_second = from_behind(lower_first, "gx", 1)
    entering = jnp.where(grp_index == 0, lower_second, lower_first)
    eastward = jnp.concatenate([entering, eastward[: length - 1]], axis=0)
    upper_first = from_behind(westward, "grp", -1)
    upper_second = from_behind(upper_first, "gx", -1)
    entering = jnp.where(grp_index == last_grp, upper_second, upper_first)
    westward = jnp.concatenate([westward[1:], entering], axis=0)
    sides = extended(post[3:5], (("gy", 2),), 1)
    northward = sides[0, :, 0:size_y]
    southward = sides[1, :, 2 : size_y + 2]
    upward = jnp.roll(post[5], 1, axis=2)
    downward = jnp.roll(post[6], -1, axis=2)
    return jnp.stack([post[0], eastward, westward, northward, southward, upward, downward])


def on_device(populations, thermal, velocity_prev, solid, phase_ids, conductivity, rates):
    padded_solid = extended(solid, (("grp", 2), ("gx", 0), ("gy", 1)), 1)
    sizes = solid.shape
    blocked = jnp.stack(
        [inner_window(padded_solid, OFFSET_TABLE[number], sizes) != 0 for number in range(27)]
    )
    fluid_cells = (solid == 0)[None]
    grp_index = lax.axis_index("grp")
    last_grp = lax.axis_size("grp") - 1
    relax_time = relaxation(phase_ids, conductivity)
    speed_brick = velocity_prev
    popul = populations
    heat_pops = thermal
    for window_number in range(WINDOWS):
        heat_brick = lax.all_to_all(
            jnp.sum(heat_pops, axis=0), "grp", split_axis=2, concat_axis=0, tiled=True
        )
        speed_column = lax.all_to_all(speed_brick, "grp", split_axis=1, concat_axis=3, tiled=True)
        for step_number in range(STEPS):
            post = collide(popul, heat_brick, rates)
            arrived = flow_arrivals(post)
            popul = jnp.where(fluid_cells, jnp.where(blocked, post[::-1], arrived), popul)
        for step_number in range(STEPS):
            heat_pops = stream_heat(
                heat_collide(heat_pops, speed_column, relax_time), grp_index, last_grp
            )
        if window_number + 1 < WINDOWS:
            speed_brick = flow_speed(popul, heat_brick, solid)
    return (popul, heat_pops)


def solution(mesh):
    in_specs = (
        P(None, "gx", "gy", "grp"),
        P(None, ("gx", "grp"), "gy", None),
        P(None, "gx", "gy", "grp"),
        P("gx", "gy", "grp"),
        P(("gx", "grp"), "gy", None),
        P(),
        P(),
    )
    out_specs = (P(None, "gx", "gy", "grp"), P(None, ("gx", "grp"), "gy", None))
    return jax.shard_map(
        on_device, mesh=mesh, in_specs=in_specs, out_specs=out_specs, check_vma=False
    )
```

profile of v0, /device:TPU:25, one launch (start us, length us, event | category | flops | bytes accessed | tf_op | source)
XLA Modules:
  0.0 329.0 jit_solution(9613565971058503574)
XLA Ops:
  4.2 8.3 %all-to-all-start = ((f32[4,1,1024]{2,1,0:T(1,128)}), f32[4,1,1024]{2,1,0:T(1,128)S(1)}, u32[]{:S(2)}, u32[]{:S(2)}) async-start(f32[4,1,1024]{2,1,0:T(1,128)} %reshape.2767), calls=%async_computation | async-start | bytes 32768 | tf_op jit(solution)/shard_map/all_to_all | solution.py:195
  12.6 2.4 collective-permute-start
  19.8 2.4 collective-permute-start.2
  22.9 4.4 %collective-permute-done.3 = s32[1,8,130]{2,1,0:T(8,128)S(1)} collective-permute-done((s32[1,8,130]{2,1,0:T(8,128)S(1)}, s32[1,8,130]{2,1,0:T(8,128)S(1)}, u32[]{:S(2)}, u32[]{:S(2)}) %collective-permute-start.3) | collective-permute-done | bytes 4192 | tf_op jit(solution)/shard_map/ppermute | solution.py:45
  27.4 2.6 collective-permute-start.4
  30.8 2.9 collective-permute-done.5
  35.4 5.3 %all-to-all-start.1 = ((f32[3,4,8,128]{3,2,0,1:T(8,128)}), f32[3,4,8,128]{3,2,0,1:T(8,128)S(1)}, u32[]{:S(2)}, u32[]{:S(2)}) async-start(f32[3,4,8,128]{3,2,0,1:T(8,128)} %copy.120), calls=%async_computation.1 | async-start | bytes 98304 | tf_op jit(solution)/shard_map/all_to_all | solution.py:198
  45.0 3.8 %collective-permute-start.7 = (f32[1,3,3,1,8,128]{5,4,3,2,1,0:T(8,128)S(1)}, f32[1,3,3,1,8,128]{5,4,3,2,1,0:T(8,128)S(1)}, u32[]{:S(2)}, u32[]{:S(2)}) collective-permute-start(f32[1,3,3,1,8,128]{5,4,3,2,1,0:T(8,128)S(1)} %slice.1604), channel_id=1, source_target_pairs={{0,4},{4,8},{8,12},{12,16},{16,20},{20,24},{24,28},{28,32},{32,36}... | collective-permute-start | bytes 110600 | tf_op jit(solution)/shard_map/ppermute | solution.py:33
  51.4 1.7 collective-permute-start.9
  54.3 2.4 collective-permute-start.30
  58.3 2.4 collective-permute-start.10
  60.9 6.8 %collective-permute-done.10 = f32[3,3,1,4,8,1]{5,4,3,2,1,0:T(8,128)S(1)} collective-permute-done((f32[3,3,1,4,8,1]{5,4,3,2,1,0:T(8,128)S(1)}, f32[3,3,1,4,8,1]{5,4,3,2,1,0:T(8,128)S(1)}, u32[]{:S(2)}, u32[]{:S(2)}) %collective-permute-start.10) | collective-permute-done | bytes 1184 | tf_op jit(solution)/shard_map/ppermute | solution.py:33
  67.7 2.6 collective-permute-start.35
  73.3 4.4 %collective-permute-start.31 = (f32[1,8,512]{2,1,0:T(8,128)S(1)}, f32[1,8,512]{2,1,0:T(8,128)S(1)}, u32[]{:S(2)}, u32[]{:S(2)}) collective-permute-start(f32[1,8,512]{2,1,0:T(8,128)S(1)} %collective-permute-done.30), channel_id=1, source_target_pairs={{0,4},{4,8},{8,12},{12,16},{16,20},{20,24},{24,28},{28,32},{32,36}... | collective-permute-start | bytes 49160 | tf_op jit(solution)/shard_map/ppermute | solution.py:33
  78.0 3.9 %collective-permute-start.13 = (f32[1,3,3,1,8,128]{5,4,3,2,1,0:T(8,128)S(1)}, f32[1,3,3,1,8,128]{5,4,3,2,1,0:T(8,128)S(1)}, u32[]{:S(2)}, u32[]{:S(2)}) collective-permute-start(f32[1,3,3,1,8,128]{5,4,3,2,1,0:T(8,128)S(1)} %slice.1622), channel_id=1, source_target_pairs={{0,4},{4,8},{8,12},{12,16},{16,20},{20,24},{24,28},{28,32},{32,36}... | collective-permute-start | bytes 110600 | tf_op jit(solution)/shard_map/ppermute | solution.py:33
  83.5 2.2 collective-permute-start.36
  85.7 10.2 %collective-permute-start.38 = (f32[1,8,512]{2,1,0:T(8,128)S(1)}, f32[1,8,512]{2,1,0:T(8,128)S(1)}, u32[]{:S(2)}, u32[]{:S(2)}) collective-permute-start(f32[1,8,512]{2,1,0:T(8,128)S(1)} %get-tuple-element.147), channel_id=1, source_target_pairs={{0,192},{64,0},{128,64},{192,128},{1,193},{65,1},{129,65},{193,129... | collective-permute-start | bytes 49160 | tf_op jit(solution)/shard_map/ppermute | solution.py:33
  96.0 3.0 collective-permute-start.14
  99.9 2.9 collective-permute-done.15
  105.9 3.1 collective-permute-start.37
  109.1 2.4 collective-permute-done.16
  117.1 2.3 collective-permute-start.42
  120.9 2.7 collective-permute-start.47
  123.6 3.9 %collective-permute-start.43 = (f32[1,8,512]{2,1,0:T(8,128)S(1)}, f32[1,8,512]{2,1,0:T(8,128)S(1)}, u32[]{:S(2)}, u32[]{:S(2)}) collective-permute-start(f32[1,8,512]{2,1,0:T(8,128)S(1)} %collective-permute-done.42), channel_id=1, source_target_pairs={{0,4},{4,8},{8,12},{12,16},{16,20},{20,24},{24,28},{28,32},{32,36}... | collective-permute-start | bytes 49160 | tf_op jit(solution)/shard_map/ppermute | solution.py:33
  128.0 3.9 %collective-permute-start.19 = (f32[1,3,3,1,8,128]{5,4,3,2,1,0:T(8,128)S(1)}, f32[1,3,3,1,8,128]{5,4,3,2,1,0:T(8,128)S(1)}, u32[]{:S(2)}, u32[]{:S(2)}) collective-permute-start(f32[1,3,3,1,8,128]{5,4,3,2,1,0:T(8,128)S(1)} %slice.1640), channel_id=1, source_target_pairs={{0,4},{4,8},{8,12},{12,16},{16,20},{20,24},{24,28},{28,32},{32,36}... | collective-permute-start | bytes 110600 | tf_op jit(solution)/shard_map/ppermute | solution.py:33
  134.5 3.0 collective-permute-start.50
  137.6 2.7 collective-permute-start.20
  141.2 2.9 collective-permute-done.21
  147.0 2.9 collective-permute-start.49
  149.9 2.0 collective-permute-done.22
  156.5 3.9 %collective-permute-start.25 = (f32[1,3,3,1,8,128]{5,4,3,2,1,0:T(8,128)S(1)}, f32[1,3,3,1,8,128]{5,4,3,2,1,0:T(8,128)S(1)}, u32[]{:S(2)}, u32[]{:S(2)}) collective-permute-start(f32[1,3,3,1,8,128]{5,4,3,2,1,0:T(8,128)S(1)} %slice.1658), channel_id=1, source_target_pairs={{0,4},{4,8},{8,12},{12,16},{16,20},{20,24},{24,28},{28,32},{32,36}... | collective-permute-start | bytes 110600 | tf_op jit(solution)/shard_map/ppermute | solution.py:33
  162.8 4.3 %all-to-all-start.2 = ((f32[4,1,1024]{2,1,0:T(1,128)}), f32[4,1,1024]{2,1,0:T(1,128)S(1)}, u32[]{:S(2)}, u32[]{:S(2)}) async-start(f32[4,1,1024]{2,1,0:T(1,128)} %reshape.2769), calls=%async_computation.2 | async-start | bytes 32768 | tf_op jit(solution)/shard_map/all_to_all | solution.py:195
  167.3 6.5 %all-to-all-done.2 = f32[4,1,1024]{2,1,0:T(1,128)S(1)} async-done(((f32[4,1,1024]{2,1,0:T(1,128)}), f32[4,1,1024]{2,1,0:T(1,128)S(1)}, u32[]{:S(2)}, u32[]{:S(2)}) %all-to-all-start.2) | async-done | bytes 16416 | tf_op jit(solution)/shard_map/all_to_all | solution.py:195
  179.5 2.0 collective-permute-start.29
  181.7 4.1 %collective-permute-done.28 = f32[3,3,1,4,8,1]{5,4,3,2,1,0:T(8,128)S(1)} collective-permute-done((f32[3,3,1,4,8,1]{5,4,3,2,1,0:T(8,128)S(1)}, f32[3,3,1,4,8,1]{5,4,3,2,1,0:T(8,128)S(1)}, u32[]{:S(2)}, u32[]{:S(2)}) %collective-permute-start.28) | collective-permute-done | bytes 1184 | tf_op jit(solution)/shard_map/ppermute | solution.py:33
  185.8 4.8 %collective-permute-done.29 = f32[3,3,1,4,8,1]{5,4,3,2,1,0:T(8,128)S(1)} collective-permute-done((f32[3,3,1,4,8,1]{5,4,3,2,1,0:T(8,128)S(1)}, f32[3,3,1,4,8,1]{5,4,3,2,1,0:T(8,128)S(1)}, u32[]{:S(2)}, u32[]{:S(2)}) %collective-permute-start.29) | collective-permute-done | bytes 1184 | tf_op jit(solution)/shard_map/ppermute | solution.py:33
  193.0 3.3 all-to-all-start.3
  198.0 3.4 %collective-permute-start.55 = (f32[1,3,3,1,8,128]{5,4,3,2,1,0:T(8,128)S(1)}, f32[1,3,3,1,8,128]{5,4,3,2,1,0:T(8,128)S(1)}, u32[]{:S(2)}, u32[]{:S(2)}) collective-permute-start(f32[1,3,3,1,8,128]{5,4,3,2,1,0:T(8,128)S(1)} %slice.1727), channel_id=1, source_target_pairs={{0,4},{4,8},{8,12},{12,16},{16,20},{20,24},{24,28},{28,32},{32,36}... | collective-permute-start | bytes 110600 | tf_op jit(solution)/shard_map/ppermute | solution.py:33
  207.3 3.6 %collective-permute-start.58 = (f32[3,3,1,4,8,1]{5,4,3,2,1,0:T(8,128)S(1)}, f32[3,3,1,4,8,1]{5,4,3,2,1,0:T(8,128)S(1)}, u32[]{:S(2)}, u32[]{:S(2)}) collective-permute-start(f32[3,3,1,4,8,1]{5,4,3,2,1,0:T(8,128)S(1)} %get-tuple-element.59), channel_id=1, source_target_pairs={{0,192},{64,0},{128,64},{192,128},{1,193},{65,1},{129,65},{193,129... | collective-permute-start | bytes 3464 | tf_op jit(solution)/shard_map/ppermute | solution.py:33
  211.0 4.4 %collective-permute-done.58 = f32[3,3,1,4,8,1]{5,4,3,2,1,0:T(8,128)S(1)} collective-permute-done((f32[3,3,1,4,8,1]{5,4,3,2,1,0:T(8,128)S(1)}, f32[3,3,1,4,8,1]{5,4,3,2,1,0:T(8,128)S(1)}, u32[]{:S(2)}, u32[]{:S(2)}) %collective-permute-start.58) | collective-permute-done | bytes 1184 | tf_op jit(solution)/shard_map/ppermute | solution.py:33
  215.4 3.0 collective-permute-done.59
  222.4 4.3 %collective-permute-start.61 = (f32[1,3,3,1,8,128]{5,4,3,2,1,0:T(8,128)S(1)}, f32[1,3,3,1,8,128]{5,4,3,2,1,0:T(8,128)S(1)}, u32[]{:S(2)}, u32[]{:S(2)}) collective-permute-start(f32[1,3,3,1,8,128]{5,4,3,2,1,0:T(8,128)S(1)} %slice.1745), channel_id=1, source_target_pairs={{0,4},{4,8},{8,12},{12,16},{16,20},{20,24},{24,28},{28,32},{32,36}... | collective-permute-start | bytes 110600 | tf_op jit(solution)/shard_map/ppermute | solution.py:33
  227.0 3.6 %collective-permute-start.80 = (f32[1,8,512]{2,1,0:T(8,128)S(1)}, f32[1,8,512]{2,1,0:T(8,128)S(1)}, u32[]{:S(2)}, u32[]{:S(2)}) collective-permute-start(f32[1,8,512]{2,1,0:T(8,128)S(1)} %get-tuple-element.124), channel_id=1, source_target_pairs={{0,192},{64,0},{128,64},{192,128},{1,193},{65,1},{129,65},{193,129... | collective-permute-start | bytes 49160 | tf_op jit(solution)/shard_map/ppermute | solution.py:33
  231.7 1.9 collective-permute-start.83
  237.6 3.0 collective-permute-done.81
  242.0 2.7 collective-permute-start.86
  247.5 3.2 collective-permute-done.64
  250.7 2.7 collective-permute-start.89
  256.4 4.3 %collective-permute-start.85 = (f32[1,8,512]{2,1,0:T(8,128)S(1)}, f32[1,8,512]{2,1,0:T(8,128)S(1)}, u32[]{:S(2)}, u32[]{:S(2)}) collective-permute-start(f32[1,8,512]{2,1,0:T(8,128)S(1)} %collective-permute-done.84), channel_id=1, source_target_pairs={{0,4},{4,8},{8,12},{12,16},{16,20},{20,24},{24,28},{28,32},{32,36}... | collective-permute-start | bytes 49160 | tf_op jit(solution)/shard_map/ppermute | solution.py:33
  261.0 3.9 %collective-permute-start.67 = (f32[1,3,3,1,8,128]{5,4,3,2,1,0:T(8,128)S(1)}, f32[1,3,3,1,8,128]{5,4,3,2,1,0:T(8,128)S(1)}, u32[]{:S(2)}, u32[]{:S(2)}) collective-permute-start(f32[1,3,3,1,8,128]{5,4,3,2,1,0:T(8,128)S(1)} %slice.1763), channel_id=1, source_target_pairs={{0,4},{4,8},{8,12},{12,16},{16,20},{20,24},{24,28},{28,32},{32,36}... | collective-permute-start | bytes 110600 | tf_op jit(solution)/shard_map/ppermute | solution.py:33
  266.5 3.4 %collective-permute-start.90 = (f32[1,8,512]{2,1,0:T(8,128)S(1)}, f32[1,8,512]{2,1,0:T(8,128)S(1)}, u32[]{:S(2)}, u32[]{:S(2)}) collective-permute-start(f32[1,8,512]{2,1,0:T(8,128)S(1)} %get-tuple-element.109), channel_id=1, source_target_pairs={{0,64},{64,128},{128,192},{192,0},{1,65},{65,129},{129,193},{193,1... | collective-permute-start | bytes 49160 | tf_op jit(solution)/shard_map/ppermute | solution.py:33
  270.2 2.7 collective-permute-start.68
  273.8 2.9 collective-permute-done.69
  277.0 2.5 collective-permute-start.70
  279.7 2.8 collective-permute-start.91
  282.7 3.9 %collective-permute-done.71 = f32[3,3,1,4,8,1]{5,4,3,2,1,0:T(8,128)S(1)} collective-permute-done((f32[3,3,1,4,8,1]{5,4,3,2,1,0:T(8,128)S(1)}, f32[3,3,1,4,8,1]{5,4,3,2,1,0:T(8,128)S(1)}, u32[]{:S(2)}, u32[]{:S(2)}) %collective-permute-start.71) | collective-permute-done | bytes 1184 | tf_op jit(solution)/shard_map/ppermute | solution.py:33
  290.0 2.3 collective-permute-start.96
  292.5 3.9 %collective-permute-start.73 = (f32[1,3,3,1,8,128]{5,4,3,2,1,0:T(8,128)S(1)}, f32[1,3,3,1,8,128]{5,4,3,2,1,0:T(8,128)S(1)}, u32[]{:S(2)}, u32[]{:S(2)}) collective-permute-start(f32[1,3,3,1,8,128]{5,4,3,2,1,0:T(8,128)S(1)} %slice.1781), channel_id=1, source_target_pairs={{0,4},{4,8},{8,12},{12,16},{16,20},{20,24},{24,28},{28,32},{32,36}... | collective-permute-start | bytes 110600 | tf_op jit(solution)/shard_map/ppermute | solution.py:33
  296.4 2.8 collective-permute-start.98
  301.7 2.1 collective-permute-start.101
  303.7 5.3 %collective-permute-done.99 = f32[1,8,512]{2,1,0:T(8,128)S(1)} collective-permute-done((f32[1,8,512]{2,1,0:T(8,128)S(1)}, f32[1,8,512]{2,1,0:T(8,128)S(1)}, u32[]{:S(2)}, u32[]{:S(2)}) %collective-permute-start.99) | collective-permute-done | bytes 16416 | tf_op jit(solution)/shard_map/ppermute | solution.py:33
  313.9 2.9 collective-permute-start.76
  316.9 6.4 %collective-permute-done.76 = f32[3,3,1,4,8,1]{5,4,3,2,1,0:T(8,128)S(1)} collective-permute-done((f32[3,3,1,4,8,1]{5,4,3,2,1,0:T(8,128)S(1)}, f32[3,3,1,4,8,1]{5,4,3,2,1,0:T(8,128)S(1)}, u32[]{:S(2)}, u32[]{:S(2)}) %collective-permute-start.76) | collective-permute-done | bytes 1184 | tf_op jit(solution)/shard_map/ppermute | solution.py:33
  323.3 4.4 %collective-permute-done.77 = f32[3,3,1,4,8,1]{5,4,3,2,1,0:T(8,128)S(1)} collective-permute-done((f32[3,3,1,4,8,1]{5,4,3,2,1,0:T(8,128)S(1)}, f32[3,3,1,4,8,1]{5,4,3,2,1,0:T(8,128)S(1)}, u32[]{:S(2)}, u32[]{:S(2)}) %collective-permute-start.77) | collective-permute-done | bytes 1184 | tf_op jit(solution)/shard_map/ppermute | solution.py:33
  (629 shorter events, 97.4 us)
Async XLA Ops:
  4.2 31.2 %all-to-all-start = ((f32[4,1,1024]{2,1,0:T(1,128)}), f32[4,1,1024]{2,1,0:T(1,128)S(1)}, u32[]{:S(2)}, u32[]{:S(2)}) async-start(f32[4,1,1024]{2,1,0:T(1,128)} %reshape.2767), calls=%async_computation | async-start | bytes 32768 | tf_op jit(solution)/shard_map/all_to_all | solution.py:195
  35.4 17.7 %all-to-all-start.1 = ((f32[3,4,8,128]{3,2,0,1:T(8,128)}), f32[3,4,8,128]{3,2,0,1:T(8,128)S(1)}, u32[]{:S(2)}, u32[]{:S(2)}) async-start(f32[3,4,8,128]{3,2,0,1:T(8,128)} %copy.120), calls=%async_computation.1 | async-start | bytes 98304 | tf_op jit(solution)/shard_map/all_to_all | solution.py:198
  54.3 19.0 %collective-permute-start.30 = (f32[1,8,512]{2,1,0:T(8,128)S(1)}, f32[1,8,512]{2,1,0:T(8,128)S(1)}, u32[]{:S(2)}, u32[]{:S(2)}) collective-permute-start(f32[1,8,512]{2,1,0:T(8,128)S(1)} %get-tuple-element.156), channel_id=1, source_target_pairs={{0,64},{64,128},{128,192},{192,0},{1,65},{65,129},{129,193},{193,1... | collective-permute-start | bytes 49160 | tf_op jit(solution)/shard_map/ppermute | solution.py:33
  56.7 21.1 %collective-permute-start.32 = (f32[1,8,512]{2,1,0:T(8,128)S(1)}, f32[1,8,512]{2,1,0:T(8,128)S(1)}, u32[]{:S(2)}, u32[]{:S(2)}) collective-permute-start(f32[1,8,512]{2,1,0:T(8,128)S(1)} %get-tuple-element.155), channel_id=1, source_target_pairs={{0,192},{64,0},{128,64},{192,128},{1,193},{65,1},{129,65},{193,129... | collective-permute-start | bytes 49160 | tf_op jit(solution)/shard_map/ppermute | solution.py:33
  58.1 19.9 %collective-permute-start.34 = (f32[2,1,1,512]{3,2,1,0:T(1,128)S(1)}, f32[2,1,1,512]{3,2,1,0:T(1,128)S(1)}, u32[]{:S(2)}, u32[]{:S(2)}) collective-permute-start(f32[2,1,1,512]{3,2,1,0:T(1,128)S(1)} %get-tuple-element.158), channel_id=1, source_target_pairs={{0,1},{1,2},{2,3},{3,0},{4,5},{5,6},{6,7},{7,4},{8,9},{9,10},{10,1... | collective-permute-start | bytes 12296 | tf_op jit(solution)/shard_map/ppermute | solution.py:43
  58.3 9.3 %collective-permute-start.10 = (f32[3,3,1,4,8,1]{5,4,3,2,1,0:T(8,128)S(1)}, f32[3,3,1,4,8,1]{5,4,3,2,1,0:T(8,128)S(1)}, u32[]{:S(2)}, u32[]{:S(2)}) collective-permute-start(f32[3,3,1,4,8,1]{5,4,3,2,1,0:T(8,128)S(1)} %get-tuple-element.91), channel_id=1, source_target_pairs={{0,192},{64,0},{128,64},{192,128},{1,193},{65,1},{129,65},{193,129... | collective-permute-start | bytes 3464 | tf_op jit(solution)/shard_map/ppermute | solution.py:33
  60.7 9.6 %collective-permute-start.11 = (f32[3,3,1,4,8,1]{5,4,3,2,1,0:T(8,128)S(1)}, f32[3,3,1,4,8,1]{5,4,3,2,1,0:T(8,128)S(1)}, u32[]{:S(2)}, u32[]{:S(2)}) collective-permute-start(f32[3,3,1,4,8,1]{5,4,3,2,1,0:T(8,128)S(1)} %get-tuple-element.92), channel_id=1, source_target_pairs={{0,64},{64,128},{128,192},{192,0},{1,65},{65,129},{129,193},{193,1... | collective-permute-start | bytes 3464 | tf_op jit(solution)/shard_map/ppermute | solution.py:33
  67.7 14.3 %collective-permute-start.35 = (f32[2,1,1,512]{3,2,1,0:T(1,128)S(1)}, f32[2,1,1,512]{3,2,1,0:T(1,128)S(1)}, u32[]{:S(2)}, u32[]{:S(2)}) collective-permute-start(f32[2,1,1,512]{3,2,1,0:T(1,128)S(1)} %get-tuple-element.157), channel_id=1, source_target_pairs={{1,0},{2,1},{3,2},{0,3},{5,4},{6,5},{7,6},{4,7},{9,8},{10,9},{11,1... | collective-permute-start | bytes 12296 | tf_op jit(solution)/shard_map/ppermute | solution.py:45
  72.9 23.0 %collective-permute-start.12 = (f32[1,3,3,1,8,128]{5,4,3,2,1,0:T(8,128)S(1)}, f32[1,3,3,1,8,128]{5,4,3,2,1,0:T(8,128)S(1)}, u32[]{:S(2)}, u32[]{:S(2)}) collective-permute-start(f32[1,3,3,1,8,128]{5,4,3,2,1,0:T(8,128)S(1)} %slice.1619), channel_id=1, source_target_pairs={{0,60},{4,0},{8,4},{12,8},{16,12},{20,16},{24,20},{28,24},{32,28},... | collective-permute-start | bytes 110600 | tf_op jit(solution)/shard_map/ppermute | solution.py:33
  73.3 8.6 %collective-permute-start.31 = (f32[1,8,512]{2,1,0:T(8,128)S(1)}, f32[1,8,512]{2,1,0:T(8,128)S(1)}, u32[]{:S(2)}, u32[]{:S(2)}) collective-permute-start(f32[1,8,512]{2,1,0:T(8,128)S(1)} %collective-permute-done.30), channel_id=1, source_target_pairs={{0,4},{4,8},{8,12},{12,16},{16,20},{20,24},{24,28},{28,32},{32,36}... | collective-permute-start | bytes 49160 | tf_op jit(solution)/shard_map/ppermute | solution.py:33
  78.0 18.0 %collective-permute-start.13 = (f32[1,3,3,1,8,128]{5,4,3,2,1,0:T(8,128)S(1)}, f32[1,3,3,1,8,128]{5,4,3,2,1,0:T(8,128)S(1)}, u32[]{:S(2)}, u32[]{:S(2)}) collective-permute-start(f32[1,3,3,1,8,128]{5,4,3,2,1,0:T(8,128)S(1)} %slice.1622), channel_id=1, source_target_pairs={{0,4},{4,8},{8,12},{12,16},{16,20},{20,24},{24,28},{28,32},{32,36}... | collective-permute-start | bytes 110600 | tf_op jit(solution)/shard_map/ppermute | solution.py:33
  83.5 22.1 %collective-permute-start.36 = (f32[1,8,512]{2,1,0:T(8,128)S(1)}, f32[1,8,512]{2,1,0:T(8,128)S(1)}, u32[]{:S(2)}, u32[]{:S(2)}) collective-permute-start(f32[1,8,512]{2,1,0:T(8,128)S(1)} %get-tuple-element.148), channel_id=1, source_target_pairs={{0,64},{64,128},{128,192},{192,0},{1,65},{65,129},{129,193},{193,1... | collective-permute-start | bytes 49160 | tf_op jit(solution)/shard_map/ppermute | solution.py:33
  85.7 20.2 %collective-permute-start.38 = (f32[1,8,512]{2,1,0:T(8,128)S(1)}, f32[1,8,512]{2,1,0:T(8,128)S(1)}, u32[]{:S(2)}, u32[]{:S(2)}) collective-permute-start(f32[1,8,512]{2,1,0:T(8,128)S(1)} %get-tuple-element.147), channel_id=1, source_target_pairs={{0,192},{64,0},{128,64},{192,128},{1,193},{65,1},{129,65},{193,129... | collective-permute-start | bytes 49160 | tf_op jit(solution)/shard_map/ppermute | solution.py:33
  96.0 19.3 %collective-permute-start.40 = (f32[2,1,1,512]{3,2,1,0:T(1,128)S(1)}, f32[2,1,1,512]{3,2,1,0:T(1,128)S(1)}, u32[]{:S(2)}, u32[]{:S(2)}) collective-permute-start(f32[2,1,1,512]{3,2,1,0:T(1,128)S(1)} %get-tuple-element.150), channel_id=1, source_target_pairs={{0,1},{1,2},{2,3},{3,0},{4,5},{5,6},{6,7},{7,4},{8,9},{9,10},{10,1... | collective-permute-start | bytes 12296 | tf_op jit(solution)/shard_map/ppermute | solution.py:43
  103.0 8.4 %collective-permute-start.16 = (f32[3,3,1,4,8,1]{5,4,3,2,1,0:T(8,128)S(1)}, f32[3,3,1,4,8,1]{5,4,3,2,1,0:T(8,128)S(1)}, u32[]{:S(2)}, u32[]{:S(2)}) collective-permute-start(f32[3,3,1,4,8,1]{5,4,3,2,1,0:T(8,128)S(1)} %get-tuple-element.83), channel_id=1, source_target_pairs={{0,192},{64,0},{128,64},{192,128},{1,193},{65,1},{129,65},{193,129... | collective-permute-start | bytes 3464 | tf_op jit(solution)/shard_map/ppermute | solution.py:33
  104.6 7.7 %collective-permute-start.17 = (f32[3,3,1,4,8,1]{5,4,3,2,1,0:T(8,128)S(1)}, f32[3,3,1,4,8,1]{5,4,3,2,1,0:T(8,128)S(1)}, u32[]{:S(2)}, u32[]{:S(2)}) collective-permute-start(f32[3,3,1,4,8,1]{5,4,3,2,1,0:T(8,128)S(1)} %get-tuple-element.84), channel_id=1, source_target_pairs={{0,64},{64,128},{128,192},{192,0},{1,65},{65,129},{129,193},{193,1... | collective-permute-start | bytes 3464 | tf_op jit(solution)/shard_map/ppermute | solution.py:33
  105.6 9.7 %collective-permute-start.41 = (f32[2,1,1,512]{3,2,1,0:T(1,128)S(1)}, f32[2,1,1,512]{3,2,1,0:T(1,128)S(1)}, u32[]{:S(2)}, u32[]{:S(2)}) collective-permute-start(f32[2,1,1,512]{3,2,1,0:T(1,128)S(1)} %get-tuple-element.149), channel_id=1, source_target_pairs={{1,0},{2,1},{3,2},{0,3},{5,4},{6,5},{7,6},{4,7},{9,8},{10,9},{11,1... | collective-permute-start | bytes 12296 | tf_op jit(solution)/shard_map/ppermute | solution.py:45
  105.9 9.4 %collective-permute-start.37 = (f32[1,8,512]{2,1,0:T(8,128)S(1)}, f32[1,8,512]{2,1,0:T(8,128)S(1)}, u32[]{:S(2)}, u32[]{:S(2)}) collective-permute-start(f32[1,8,512]{2,1,0:T(8,128)S(1)} %collective-permute-done.36), channel_id=1, source_target_pairs={{0,4},{4,8},{8,12},{12,16},{16,20},{20,24},{24,28},{28,32},{32,36}... | collective-permute-start | bytes 49160 | tf_op jit(solution)/shard_map/ppermute | solution.py:33
  115.1 22.4 %collective-permute-start.18 = (f32[1,3,3,1,8,128]{5,4,3,2,1,0:T(8,128)S(1)}, f32[1,3,3,1,8,128]{5,4,3,2,1,0:T(8,128)S(1)}, u32[]{:S(2)}, u32[]{:S(2)}) collective-permute-start(f32[1,3,3,1,8,128]{5,4,3,2,1,0:T(8,128)S(1)} %slice.1637), channel_id=1, source_target_pairs={{0,60},{4,0},{8,4},{12,8},{16,12},{20,16},{24,20},{28,24},{32,28},... | collective-permute-start | bytes 110600 | tf_op jit(solution)/shard_map/ppermute | solution.py:33
  119.4 8.1 %collective-permute-start.44 = (f32[1,8,512]{2,1,0:T(8,128)S(1)}, f32[1,8,512]{2,1,0:T(8,128)S(1)}, u32[]{:S(2)}, u32[]{:S(2)}) collective-permute-start(f32[1,8,512]{2,1,0:T(8,128)S(1)} %get-tuple-element.139), channel_id=1, source_target_pairs={{0,192},{64,0},{128,64},{192,128},{1,193},{65,1},{129,65},{193,129... | collective-permute-start | bytes 49160 | tf_op jit(solution)/shard_map/ppermute | solution.py:33
  120.7 7.2 %collective-permute-start.46 = (f32[2,1,1,512]{3,2,1,0:T(1,128)S(1)}, f32[2,1,1,512]{3,2,1,0:T(1,128)S(1)}, u32[]{:S(2)}, u32[]{:S(2)}) collective-permute-start(f32[2,1,1,512]{3,2,1,0:T(1,128)S(1)} %get-tuple-element.142), channel_id=1, source_target_pairs={{0,1},{1,2},{2,3},{3,0},{4,5},{5,6},{6,7},{7,4},{8,9},{9,10},{10,1... | collective-permute-start | bytes 12296 | tf_op jit(solution)/shard_map/ppermute | solution.py:43
  120.9 10.9 %collective-permute-start.47 = (f32[2,1,1,512]{3,2,1,0:T(1,128)S(1)}, f32[2,1,1,512]{3,2,1,0:T(1,128)S(1)}, u32[]{:S(2)}, u32[]{:S(2)}) collective-permute-start(f32[2,1,1,512]{3,2,1,0:T(1,128)S(1)} %get-tuple-element.141), channel_id=1, source_target_pairs={{1,0},{2,1},{3,2},{0,3},{5,4},{6,5},{7,6},{4,7},{9,8},{10,9},{11,1... | collective-permute-start | bytes 12296 | tf_op jit(solution)/shard_map/ppermute | solution.py:45
  123.6 8.2 %collective-permute-start.43 = (f32[1,8,512]{2,1,0:T(8,128)S(1)}, f32[1,8,512]{2,1,0:T(8,128)S(1)}, u32[]{:S(2)}, u32[]{:S(2)}) collective-permute-start(f32[1,8,512]{2,1,0:T(8,128)S(1)} %collective-permute-done.42), channel_id=1, source_target_pairs={{0,4},{4,8},{8,12},{12,16},{16,20},{20,24},{24,28},{28,32},{32,36}... | collective-permute-start | bytes 49160 | tf_op jit(solution)/shard_map/ppermute | solution.py:33
  128.0 9.6 %collective-permute-start.19 = (f32[1,3,3,1,8,128]{5,4,3,2,1,0:T(8,128)S(1)}, f32[1,3,3,1,8,128]{5,4,3,2,1,0:T(8,128)S(1)}, u32[]{:S(2)}, u32[]{:S(2)}) collective-permute-start(f32[1,3,3,1,8,128]{5,4,3,2,1,0:T(8,128)S(1)} %slice.1640), channel_id=1, source_target_pairs={{0,4},{4,8},{8,12},{12,16},{16,20},{20,24},{24,28},{28,32},{32,36}... | collective-permute-start | bytes 110600 | tf_op jit(solution)/shard_map/ppermute | solution.py:33
  133.9 13.0 %collective-permute-start.48 = (f32[1,8,512]{2,1,0:T(8,128)S(1)}, f32[1,8,512]{2,1,0:T(8,128)S(1)}, u32[]{:S(2)}, u32[]{:S(2)}) collective-permute-start(f32[1,8,512]{2,1,0:T(8,128)S(1)} %get-tuple-element.134), channel_id=1, source_target_pairs={{0,64},{64,128},{128,192},{192,0},{1,65},{65,129},{129,193},{193,1... | collective-permute-start | bytes 49160 | tf_op jit(solution)/shard_map/ppermute | solution.py:33
  134.5 12.5 %collective-permute-start.50 = (f32[1,8,512]{2,1,0:T(8,128)S(1)}, f32[1,8,512]{2,1,0:T(8,128)S(1)}, u32[]{:S(2)}, u32[]{:S(2)}) collective-permute-start(f32[1,8,512]{2,1,0:T(8,128)S(1)} %get-tuple-element.131), channel_id=1, source_target_pairs={{0,192},{64,0},{128,64},{192,128},{1,193},{65,1},{129,65},{193,129... | collective-permute-start | bytes 49160 | tf_op jit(solution)/shard_map/ppermute | solution.py:33
  137.5 19.0 %collective-permute-start.52 = (f32[2,1,1,512]{3,2,1,0:T(1,128)S(1)}, f32[2,1,1,512]{3,2,1,0:T(1,128)S(1)}, u32[]{:S(2)}, u32[]{:S(2)}) collective-permute-start(f32[2,1,1,512]{3,2,1,0:T(1,128)S(1)} %get-tuple-element.130), channel_id=1, source_target_pairs={{0,1},{1,2},{2,3},{3,0},{4,5},{5,6},{6,7},{7,4},{8,9},{9,10},{10,1... | collective-permute-start | bytes 12296 | tf_op jit(solution)/shard_map/ppermute | solution.py:43
  144.3 7.7 %collective-permute-start.22 = (f32[3,3,1,4,8,1]{5,4,3,2,1,0:T(8,128)S(1)}, f32[3,3,1,4,8,1]{5,4,3,2,1,0:T(8,128)S(1)}, u32[]{:S(2)}, u32[]{:S(2)}) collective-permute-start(f32[3,3,1,4,8,1]{5,4,3,2,1,0:T(8,128)S(1)} %get-tuple-element.75), channel_id=1, source_target_pairs={{0,192},{64,0},{128,64},{192,128},{1,193},{65,1},{129,65},{193,129... | collective-permute-start | bytes 3464 | tf_op jit(solution)/shard_map/ppermute | solution.py:33
  145.7 7.6 %collective-permute-start.23 = (f32[3,3,1,4,8,1]{5,4,3,2,1,0:T(8,128)S(1)}, f32[3,3,1,4,8,1]{5,4,3,2,1,0:T(8,128)S(1)}, u32[]{:S(2)}, u32[]{:S(2)}) collective-permute-start(f32[3,3,1,4,8,1]{5,4,3,2,1,0:T(8,128)S(1)} %get-tuple-element.76), channel_id=1, source_target_pairs={{0,64},{64,128},{128,192},{192,0},{1,65},{65,129},{129,193},{193,1... | collective-permute-start | bytes 3464 | tf_op jit(solution)/shard_map/ppermute | solution.py:33
  146.9 13.6 %collective-permute-start.53 = (f32[2,1,1,512]{3,2,1,0:T(1,128)S(1)}, f32[2,1,1,512]{3,2,1,0:T(1,128)S(1)}, u32[]{:S(2)}, u32[]{:S(2)}) collective-permute-start(f32[2,1,1,512]{3,2,1,0:T(1,128)S(1)} %get-tuple-element.129), channel_id=1, source_target_pairs={{1,0},{2,1},{3,2},{0,3},{5,4},{6,5},{7,6},{4,7},{9,8},{10,9},{11,1... | collective-permute-start | bytes 12296 | tf_op jit(solution)/shard_map/ppermute | solution.py:45
  147.0 13.5 %collective-permute-start.49 = (f32[1,8,512]{2,1,0:T(8,128)S(1)}, f32[1,8,512]{2,1,0:T(8,128)S(1)}, u32[]{:S(2)}, u32[]{:S(2)}) collective-permute-start(f32[1,8,512]{2,1,0:T(8,128)S(1)} %collective-permute-done.48), channel_id=1, source_target_pairs={{0,4},{4,8},{8,12},{12,16},{16,20},{20,24},{24,28},{28,32},{32,36}... | collective-permute-start | bytes 49160 | tf_op jit(solution)/shard_map/ppermute | solution.py:33
  152.0 8.5 %collective-permute-start.51 = (f32[1,8,512]{2,1,0:T(8,128)S(1)}, f32[1,8,512]{2,1,0:T(8,128)S(1)}, u32[]{:S(2)}, u32[]{:S(2)}) collective-permute-start(f32[1,8,512]{2,1,0:T(8,128)S(1)} %collective-permute-done.50), channel_id=1, source_target_pairs={{0,60},{4,0},{8,4},{12,8},{16,12},{20,16},{24,20},{28,24},{32,28},... | collective-permute-start | bytes 49160 | tf_op jit(solution)/shard_map/ppermute | solution.py:33
  156.1 18.8 %collective-permute-start.24 = (f32[1,3,3,1,8,128]{5,4,3,2,1,0:T(8,128)S(1)}, f32[1,3,3,1,8,128]{5,4,3,2,1,0:T(8,128)S(1)}, u32[]{:S(2)}, u32[]{:S(2)}) collective-permute-start(f32[1,3,3,1,8,128]{5,4,3,2,1,0:T(8,128)S(1)} %slice.1655), channel_id=1, source_target_pairs={{0,60},{4,0},{8,4},{12,8},{16,12},{20,16},{24,20},{28,24},{32,28},... | collective-permute-start | bytes 110600 | tf_op jit(solution)/shard_map/ppermute | solution.py:33
  156.5 18.3 %collective-permute-start.25 = (f32[1,3,3,1,8,128]{5,4,3,2,1,0:T(8,128)S(1)}, f32[1,3,3,1,8,128]{5,4,3,2,1,0:T(8,128)S(1)}, u32[]{:S(2)}, u32[]{:S(2)}) collective-permute-start(f32[1,3,3,1,8,128]{5,4,3,2,1,0:T(8,128)S(1)} %slice.1658), channel_id=1, source_target_pairs={{0,4},{4,8},{8,12},{12,16},{16,20},{20,24},{24,28},{28,32},{32,36}... | collective-permute-start | bytes 110600 | tf_op jit(solution)/shard_map/ppermute | solution.py:33
  162.8 11.0 %all-to-all-start.2 = ((f32[4,1,1024]{2,1,0:T(1,128)}), f32[4,1,1024]{2,1,0:T(1,128)S(1)}, u32[]{:S(2)}, u32[]{:S(2)}) async-start(f32[4,1,1024]{2,1,0:T(1,128)} %reshape.2769), calls=%async_computation.2 | async-start | bytes 32768 | tf_op jit(solution)/shard_map/all_to_all | solution.py:195
  179.5 11.1 %collective-permute-start.29 = (f32[3,3,1,4,8,1]{5,4,3,2,1,0:T(8,128)S(1)}, f32[3,3,1,4,8,1]{5,4,3,2,1,0:T(8,128)S(1)}, u32[]{:S(2)}, u32[]{:S(2)}) collective-permute-start(f32[3,3,1,4,8,1]{5,4,3,2,1,0:T(8,128)S(1)} %get-tuple-element.68), channel_id=1, source_target_pairs={{0,64},{64,128},{128,192},{192,0},{1,65},{65,129},{129,193},{193,1... | collective-permute-start | bytes 3464 | tf_op jit(solution)/shard_map/ppermute | solution.py:33
  193.0 33.7 %all-to-all-start.3 = ((f32[3,4,8,128]{3,2,0,1:T(8,128)}), f32[3,4,8,128]{3,2,0,1:T(8,128)S(1)}, u32[]{:S(2)}, u32[]{:S(2)}) async-start(f32[3,4,8,128]{3,2,0,1:T(8,128)} %fusion.128), calls=%async_computation.3 | async-start | bytes 98304 | tf_op jit(solution)/shard_map/all_to_all | solution.py:198
  207.3 8.1 %collective-permute-start.58 = (f32[3,3,1,4,8,1]{5,4,3,2,1,0:T(8,128)S(1)}, f32[3,3,1,4,8,1]{5,4,3,2,1,0:T(8,128)S(1)}, u32[]{:S(2)}, u32[]{:S(2)}) collective-permute-start(f32[3,3,1,4,8,1]{5,4,3,2,1,0:T(8,128)S(1)} %get-tuple-element.59), channel_id=1, source_target_pairs={{0,192},{64,0},{128,64},{192,128},{1,193},{65,1},{129,65},{193,129... | collective-permute-start | bytes 3464 | tf_op jit(solution)/shard_map/ppermute | solution.py:33
  210.9 7.5 %collective-permute-start.59 = (f32[3,3,1,4,8,1]{5,4,3,2,1,0:T(8,128)S(1)}, f32[3,3,1,4,8,1]{5,4,3,2,1,0:T(8,128)S(1)}, u32[]{:S(2)}, u32[]{:S(2)}) collective-permute-start(f32[3,3,1,4,8,1]{5,4,3,2,1,0:T(8,128)S(1)} %get-tuple-element.60), channel_id=1, source_target_pairs={{0,64},{64,128},{128,192},{192,0},{1,65},{65,129},{129,193},{193,1... | collective-permute-start | bytes 3464 | tf_op jit(solution)/shard_map/ppermute | solution.py:33
  221.2 14.1 %collective-permute-start.60 = (f32[1,3,3,1,8,128]{5,4,3,2,1,0:T(8,128)S(1)}, f32[1,3,3,1,8,128]{5,4,3,2,1,0:T(8,128)S(1)}, u32[]{:S(2)}, u32[]{:S(2)}) collective-permute-start(f32[1,3,3,1,8,128]{5,4,3,2,1,0:T(8,128)S(1)} %slice.1742), channel_id=1, source_target_pairs={{0,60},{4,0},{8,4},{12,8},{16,12},{20,16},{24,20},{28,24},{32,28},... | collective-permute-start | bytes 110600 | tf_op jit(solution)/shard_map/ppermute | solution.py:33
  222.4 12.9 %collective-permute-start.61 = (f32[1,3,3,1,8,128]{5,4,3,2,1,0:T(8,128)S(1)}, f32[1,3,3,1,8,128]{5,4,3,2,1,0:T(8,128)S(1)}, u32[]{:S(2)}, u32[]{:S(2)}) collective-permute-start(f32[1,3,3,1,8,128]{5,4,3,2,1,0:T(8,128)S(1)} %slice.1745), channel_id=1, source_target_pairs={{0,4},{4,8},{8,12},{12,16},{16,20},{20,24},{24,28},{28,32},{32,36}... | collective-permute-start | bytes 110600 | tf_op jit(solution)/shard_map/ppermute | solution.py:33
  236.1 8.7 %collective-permute-start.62 = (f32[3,1,3,4,1,128]{5,4,3,2,1,0:T(1,128)S(1)}, f32[3,1,3,4,1,128]{5,4,3,2,1,0:T(1,128)S(1)}, u32[]{:S(2)}, u32[]{:S(2)}) collective-permute-start(f32[3,1,3,4,1,128]{5,4,3,2,1,0:T(1,128)S(1)} %get-tuple-element.55), channel_id=1, source_target_pairs={{0,3},{1,0},{2,1},{3,2},{4,7},{5,4},{6,5},{7,6},{8,11},{9,8},{10,9... | collective-permute-start | bytes 55304 | tf_op jit(solution)/shard_map/ppermute | solution.py:33
  236.1 8.7 %collective-permute-start.63 = (f32[3,1,3,4,1,128]{5,4,3,2,1,0:T(1,128)S(1)}, f32[3,1,3,4,1,128]{5,4,3,2,1,0:T(1,128)S(1)}, u32[]{:S(2)}, u32[]{:S(2)}) collective-permute-start(f32[3,1,3,4,1,128]{5,4,3,2,1,0:T(1,128)S(1)} %get-tuple-element.56), channel_id=1, source_target_pairs={{0,1},{1,2},{2,3},{3,0},{4,5},{5,6},{6,7},{7,4},{8,9},{9,10},{10,1... | collective-permute-start | bytes 55304 | tf_op jit(solution)/shard_map/ppermute | solution.py:33
  241.0 15.3 %collective-permute-start.84 = (f32[1,8,512]{2,1,0:T(8,128)S(1)}, f32[1,8,512]{2,1,0:T(8,128)S(1)}, u32[]{:S(2)}, u32[]{:S(2)}) collective-permute-start(f32[1,8,512]{2,1,0:T(8,128)S(1)} %get-tuple-element.117), channel_id=1, source_target_pairs={{0,64},{64,128},{128,192},{192,0},{1,65},{65,129},{129,193},{193,1... | collective-permute-start | bytes 49160 | tf_op jit(solution)/shard_map/ppermute | solution.py:33
  242.0 18.7 %collective-permute-start.86 = (f32[1,8,512]{2,1,0:T(8,128)S(1)}, f32[1,8,512]{2,1,0:T(8,128)S(1)}, u32[]{:S(2)}, u32[]{:S(2)}) collective-permute-start(f32[1,8,512]{2,1,0:T(8,128)S(1)} %get-tuple-element.116), channel_id=1, source_target_pairs={{0,192},{64,0},{128,64},{192,128},{1,193},{65,1},{129,65},{193,129... | collective-permute-start | bytes 49160 | tf_op jit(solution)/shard_map/ppermute | solution.py:33
  244.7 16.2 %collective-permute-start.88 = (f32[2,1,1,512]{3,2,1,0:T(1,128)S(1)}, f32[2,1,1,512]{3,2,1,0:T(1,128)S(1)}, u32[]{:S(2)}, u32[]{:S(2)}) collective-permute-start(f32[2,1,1,512]{3,2,1,0:T(1,128)S(1)} %get-tuple-element.119), channel_id=1, source_target_pairs={{0,1},{1,2},{2,3},{3,0},{4,5},{5,6},{6,7},{7,4},{8,9},{9,10},{10,1... | collective-permute-start | bytes 12296 | tf_op jit(solution)/shard_map/ppermute | solution.py:43
  246.3 7.2 %collective-permute-start.65 = (f32[3,3,1,4,8,1]{5,4,3,2,1,0:T(8,128)S(1)}, f32[3,3,1,4,8,1]{5,4,3,2,1,0:T(8,128)S(1)}, u32[]{:S(2)}, u32[]{:S(2)}) collective-permute-start(f32[3,3,1,4,8,1]{5,4,3,2,1,0:T(8,128)S(1)} %get-tuple-element.52), channel_id=1, source_target_pairs={{0,64},{64,128},{128,192},{192,0},{1,65},{65,129},{129,193},{193,1... | collective-permute-start | bytes 3464 | tf_op jit(solution)/shard_map/ppermute | solution.py:33
  250.7 14.2 %collective-permute-start.89 = (f32[2,1,1,512]{3,2,1,0:T(1,128)S(1)}, f32[2,1,1,512]{3,2,1,0:T(1,128)S(1)}, u32[]{:S(2)}, u32[]{:S(2)}) collective-permute-start(f32[2,1,1,512]{3,2,1,0:T(1,128)S(1)} %get-tuple-element.118), channel_id=1, source_target_pairs={{1,0},{2,1},{3,2},{0,3},{5,4},{6,5},{7,6},{4,7},{9,8},{10,9},{11,1... | collective-permute-start | bytes 12296 | tf_op jit(solution)/shard_map/ppermute | solution.py:45
  256.2 14.0 %collective-permute-start.66 = (f32[1,3,3,1,8,128]{5,4,3,2,1,0:T(8,128)S(1)}, f32[1,3,3,1,8,128]{5,4,3,2,1,0:T(8,128)S(1)}, u32[]{:S(2)}, u32[]{:S(2)}) collective-permute-start(f32[1,3,3,1,8,128]{5,4,3,2,1,0:T(8,128)S(1)} %slice.1760), channel_id=1, source_target_pairs={{0,60},{4,0},{8,4},{12,8},{16,12},{20,16},{24,20},{28,24},{32,28},... | collective-permute-start | bytes 110600 | tf_op jit(solution)/shard_map/ppermute | solution.py:33
  256.4 8.5 %collective-permute-start.85 = (f32[1,8,512]{2,1,0:T(8,128)S(1)}, f32[1,8,512]{2,1,0:T(8,128)S(1)}, u32[]{:S(2)}, u32[]{:S(2)}) collective-permute-start(f32[1,8,512]{2,1,0:T(8,128)S(1)} %collective-permute-done.84), channel_id=1, source_target_pairs={{0,4},{4,8},{8,12},{12,16},{16,20},{20,24},{24,28},{28,32},{32,36}... | collective-permute-start | bytes 49160 | tf_op jit(solution)/shard_map/ppermute | solution.py:33
  261.0 9.2 %collective-permute-start.67 = (f32[1,3,3,1,8,128]{5,4,3,2,1,0:T(8,128)S(1)}, f32[1,3,3,1,8,128]{5,4,3,2,1,0:T(8,128)S(1)}, u32[]{:S(2)}, u32[]{:S(2)}) collective-permute-start(f32[1,3,3,1,8,128]{5,4,3,2,1,0:T(8,128)S(1)} %slice.1763), channel_id=1, source_target_pairs={{0,4},{4,8},{8,12},{12,16},{16,20},{20,24},{24,28},{28,32},{32,36}... | collective-permute-start | bytes 110600 | tf_op jit(solution)/shard_map/ppermute | solution.py:33
  266.5 13.2 %collective-permute-start.90 = (f32[1,8,512]{2,1,0:T(8,128)S(1)}, f32[1,8,512]{2,1,0:T(8,128)S(1)}, u32[]{:S(2)}, u32[]{:S(2)}) collective-permute-start(f32[1,8,512]{2,1,0:T(8,128)S(1)} %get-tuple-element.109), channel_id=1, source_target_pairs={{0,64},{64,128},{128,192},{192,0},{1,65},{65,129},{129,193},{193,1... | collective-permute-start | bytes 49160 | tf_op jit(solution)/shard_map/ppermute | solution.py:33
  269.9 9.8 %collective-permute-start.92 = (f32[1,8,512]{2,1,0:T(8,128)S(1)}, f32[1,8,512]{2,1,0:T(8,128)S(1)}, u32[]{:S(2)}, u32[]{:S(2)}) collective-permute-start(f32[1,8,512]{2,1,0:T(8,128)S(1)} %get-tuple-element.108), channel_id=1, source_target_pairs={{0,192},{64,0},{128,64},{192,128},{1,193},{65,1},{129,65},{193,129... | collective-permute-start | bytes 49160 | tf_op jit(solution)/shard_map/ppermute | solution.py:33
  270.2 19.4 %collective-permute-start.94 = (f32[2,1,1,512]{3,2,1,0:T(1,128)S(1)}, f32[2,1,1,512]{3,2,1,0:T(1,128)S(1)}, u32[]{:S(2)}, u32[]{:S(2)}) collective-permute-start(f32[2,1,1,512]{3,2,1,0:T(1,128)S(1)} %get-tuple-element.111), channel_id=1, source_target_pairs={{0,1},{1,2},{2,3},{3,0},{4,5},{5,6},{6,7},{7,4},{8,9},{9,10},{10,1... | collective-permute-start | bytes 12296 | tf_op jit(solution)/shard_map/ppermute | solution.py:43
  279.5 7.2 %collective-permute-start.71 = (f32[3,3,1,4,8,1]{5,4,3,2,1,0:T(8,128)S(1)}, f32[3,3,1,4,8,1]{5,4,3,2,1,0:T(8,128)S(1)}, u32[]{:S(2)}, u32[]{:S(2)}) collective-permute-start(f32[3,3,1,4,8,1]{5,4,3,2,1,0:T(8,128)S(1)} %get-tuple-element.44), channel_id=1, source_target_pairs={{0,64},{64,128},{128,192},{192,0},{1,65},{65,129},{129,193},{193,1... | collective-permute-start | bytes 3464 | tf_op jit(solution)/shard_map/ppermute | solution.py:33
  279.6 10.0 %collective-permute-start.95 = (f32[2,1,1,512]{3,2,1,0:T(1,128)S(1)}, f32[2,1,1,512]{3,2,1,0:T(1,128)S(1)}, u32[]{:S(2)}, u32[]{:S(2)}) collective-permute-start(f32[2,1,1,512]{3,2,1,0:T(1,128)S(1)} %get-tuple-element.110), channel_id=1, source_target_pairs={{1,0},{2,1},{3,2},{0,3},{5,4},{6,5},{7,6},{4,7},{9,8},{10,9},{11,1... | collective-permute-start | bytes 12296 | tf_op jit(solution)/shard_map/ppermute | solution.py:45
  279.7 9.9 %collective-permute-start.91 = (f32[1,8,512]{2,1,0:T(8,128)S(1)}, f32[1,8,512]{2,1,0:T(8,128)S(1)}, u32[]{:S(2)}, u32[]{:S(2)}) collective-permute-start(f32[1,8,512]{2,1,0:T(8,128)S(1)} %collective-permute-done.90), channel_id=1, source_target_pairs={{0,4},{4,8},{8,12},{12,16},{16,20},{20,24},{24,28},{28,32},{32,36}... | collective-permute-start | bytes 49160 | tf_op jit(solution)/shard_map/ppermute | solution.py:33
  289.4 19.8 %collective-permute-start.72 = (f32[1,3,3,1,8,128]{5,4,3,2,1,0:T(8,128)S(1)}, f32[1,3,3,1,8,128]{5,4,3,2,1,0:T(8,128)S(1)}, u32[]{:S(2)}, u32[]{:S(2)}) collective-permute-start(f32[1,3,3,1,8,128]{5,4,3,2,1,0:T(8,128)S(1)} %slice.1778), channel_id=1, source_target_pairs={{0,60},{4,0},{8,4},{12,8},{16,12},{20,16},{24,20},{28,24},{32,28},... | collective-permute-start | bytes 110600 | tf_op jit(solution)/shard_map/ppermute | solution.py:33
  290.0 9.2 %collective-permute-start.96 = (f32[1,8,512]{2,1,0:T(8,128)S(1)}, f32[1,8,512]{2,1,0:T(8,128)S(1)}, u32[]{:S(2)}, u32[]{:S(2)}) collective-permute-start(f32[1,8,512]{2,1,0:T(8,128)S(1)} %get-tuple-element.100), channel_id=1, source_target_pairs={{0,64},{64,128},{128,192},{192,0},{1,65},{65,129},{129,193},{193,1... | collective-permute-start | bytes 49160 | tf_op jit(solution)/shard_map/ppermute | solution.py:33
  292.5 16.7 %collective-permute-start.73 = (f32[1,3,3,1,8,128]{5,4,3,2,1,0:T(8,128)S(1)}, f32[1,3,3,1,8,128]{5,4,3,2,1,0:T(8,128)S(1)}, u32[]{:S(2)}, u32[]{:S(2)}) collective-permute-start(f32[1,3,3,1,8,128]{5,4,3,2,1,0:T(8,128)S(1)} %slice.1781), channel_id=1, source_target_pairs={{0,4},{4,8},{8,12},{12,16},{16,20},{20,24},{24,28},{28,32},{32,36}... | collective-permute-start | bytes 110600 | tf_op jit(solution)/shard_map/ppermute | solution.py:33
  300.9 8.1 %collective-permute-start.100 = (f32[2,1,1,512]{3,2,1,0:T(1,128)S(1)}, f32[2,1,1,512]{3,2,1,0:T(1,128)S(1)}, u32[]{:S(2)}, u32[]{:S(2)}) collective-permute-start(f32[2,1,1,512]{3,2,1,0:T(1,128)S(1)} %get-tuple-element.103), channel_id=1, source_target_pairs={{0,1},{1,2},{2,3},{3,0},{4,5},{5,6},{6,7},{7,4},{8,9},{9,10},{10,1... | collective-permute-start | bytes 12296 | tf_op jit(solution)/shard_map/ppermute | solution.py:43
  301.7 7.4 %collective-permute-start.101 = (f32[2,1,1,512]{3,2,1,0:T(1,128)S(1)}, f32[2,1,1,512]{3,2,1,0:T(1,128)S(1)}, u32[]{:S(2)}, u32[]{:S(2)}) collective-permute-start(f32[2,1,1,512]{3,2,1,0:T(1,128)S(1)} %get-tuple-element.102), channel_id=1, source_target_pairs={{1,0},{2,1},{3,2},{0,3},{5,4},{6,5},{7,6},{4,7},{9,8},{10,9},{11,1... | collective-permute-start | bytes 12296 | tf_op jit(solution)/shard_map/ppermute | solution.py:45
  313.9 9.4 %collective-permute-start.76 = (f32[3,3,1,4,8,1]{5,4,3,2,1,0:T(8,128)S(1)}, f32[3,3,1,4,8,1]{5,4,3,2,1,0:T(8,128)S(1)}, u32[]{:S(2)}, u32[]{:S(2)}) collective-permute-start(f32[3,3,1,4,8,1]{5,4,3,2,1,0:T(8,128)S(1)} %get-tuple-element.35), channel_id=1, source_target_pairs={{0,192},{64,0},{128,64},{192,128},{1,193},{65,1},{129,65},{193,129... | collective-permute-start | bytes 3464 | tf_op jit(solution)/shard_map/ppermute | solution.py:33
  316.8 11.0 %collective-permute-start.77 = (f32[3,3,1,4,8,1]{5,4,3,2,1,0:T(8,128)S(1)}, f32[3,3,1,4,8,1]{5,4,3,2,1,0:T(8,128)S(1)}, u32[]{:S(2)}, u32[]{:S(2)}) collective-permute-start(f32[3,3,1,4,8,1]{5,4,3,2,1,0:T(8,128)S(1)} %get-tuple-element.36), channel_id=1, source_target_pairs={{0,64},{64,128},{128,192},{192,0},{1,65},{65,129},{129,193},{193,1... | collective-permute-start | bytes 3464 | tf_op jit(solution)/shard_map/ppermute | solution.py:33
  (65 other events, 260.7 us)
where the time goes:
time: 334 us; the launch traced here: 329 us
  starting transfers between devices  179 us (54%)
  waiting for transfers between devices  98 us (29%)
  local copies, waits for them, and re-layouts  19.6 us (6%)
  other arithmetic  15.2 us (5%)
  matrix products  13.7 us (4%)
  between operations  3.8 us (1%)
    ppermute x80, starting transfers between devices, from_behind(): return lax.ppermute(value, axis, pairs)  136 us
    ppermute x80, waiting for transfers between devices, from_behind(): return lax.ppermute(value, axis, pairs)  82.4 us
    ppermute x11, starting transfers between devices, extended(): lax.ppermute(head, axis, [((i + 1) % count, i) for i in range(count)])  16.3 us
    unnamed x131, local copies, waits for them, and re-layouts  14.8 us
    all_to_all x2, starting transfers between devices, on_device(): lax.all_to_all(jnp.sum(heat_pops, axis=0), 'grp', split_axis=2, concat_ax...  12.6 us
    all_to_all x2, starting transfers between devices, on_device(): lax.all_to_all(speed_brick, 'grp', split_axis=1, concat_axis=3, tiled=True)  8.57 us
  transfers between devices with their start and end apart: 106, of which 41 were waited for; matrix products, arithmetic and copies ran while one was open for 11% of the time, Pallas kernels for 0%

commit v1 on v0

v1 whole, which is shorter than its diff:
```python
import functools

import jax
import jax.numpy as jnp
import numpy as np
from jax import lax
from jax.experimental import pallas as pl
from jax.experimental.pallas import tpu as pltpu
from jax.sharding import PartitionSpec as P

STEPS = 4
WINDOWS = 2
BUOYANCY = 0.03
REFERENCE_HEAT = 1.0
MESH = pl.DeviceIdType.MESH
F32 = jnp.float32

RING = [(-1, -1), (-1, 0), "x-", (-1, 1), (0, 1), "y+", (1, 1), (1, 0), "x+", (1, -1), (0, -1), "y-", (0, 0), "0", "z+", "z-"]
THERMAL = {"0": (0, 0, 0), "x+": (1, 0, 0), "x-": (-1, 0, 0), "y+": (0, 1, 0), "y-": (0, -1, 0), "z+": (0, 0, 1), "z-": (0, 0, -1)}
HEAT_ORDER = ["0", "x+", "x-", "y+", "y-", "z+", "z-"]
VELOCITY = []
FLOW_AT = {}
HEAT_AT = {}
for entry in RING:
    if isinstance(entry, str):
        HEAT_AT[HEAT_ORDER.index(entry)] = len(VELOCITY)
        VELOCITY.append(THERMAL[entry])
    else:
        for c in (-1, 0, 1):
            FLOW_AT[entry + (c,)] = len(VELOCITY)
            VELOCITY.append(entry + (c,))
COUNT = len(VELOCITY)
FLOW = [(a, b, c) for a in (-1, 0, 1) for b in (-1, 0, 1) for c in (-1, 0, 1)]
X_GROUP = {1: (14, 24), -1: (0, 10)}
Y_GROUP = {1: [(7, 17)], -1: [(21, 28), (0, 3)]}
EDGE_GROUP = {(-1, -1): (0, 3), (-1, 1): (7, 10), (1, 1): (14, 17), (1, -1): (21, 24)}
X_SLOT, XH_SLOT, H_SLOT = 0, 1, 6
PLANES = 4
ROW = 8
SOURCE_ROW = {1: (15, 7), -1: (8, 16)}


def center(plane):
    return 32 * (plane + 1) % 128


def slot_of(a, plane):
    if plane < 0 or plane >= PLANES:
        return X_SLOT
    return 2 + (plane if a >= 0 else PLANES - 1 - plane)


def turn(value, amount):
    amount = amount % 128
    return pltpu.roll(value, amount, 1) if amount else value


MESSAGES = []
for (a, b), span in EDGE_GROUP.items():
    s, t = SOURCE_ROW[b]
    MESSAGES.append(((0, a, b), span, (5, 7), (0, 2), (s, s + 1), (t, t + 1)))
FIRST_X = len(MESSAGES)
for a in (1, -1):
    MESSAGES.append(((0, a, 0), X_GROUP[a], (5, 7), (0, 2), (ROW, ROW + 8), (ROW, ROW + 8)))
FIRST_Y = len(MESSAGES)
for b in (1, -1):
    s, t = SOURCE_ROW[b]
    for span in Y_GROUP[b]:
        MESSAGES.append(((0, 0, b), span, (2, 7), (2, 7), (s, s + 1), (t, t + 1)))

RELAXED = [m for m in [(p, q, r) for p in range(3) for q in range(3) for r in range(3)] if m not in ((0, 0, 0), (0, 0, 1), (0, 1, 0), (1, 0, 0))]
COEF = {}
for m in RELAXED:
    COEF[m, "keep"] = len(COEF)
    if m != (1, 1, 1):
        COEF[m, "gain"] = len(COEF)


def gain_scale(m):
    odd = sum(v == 1 for v in m)
    two = sum(v == 2 for v in m)
    return 3.0 ** (-(max(two - 1, 0) if odd == 0 else two))


def collide_flow(f, heat, coef):
    for axis in range(3):
        g = {}
        for one in (-1, 0, 1):
            for two in (-1, 0, 1):
                def at(v):
                    key = [one, two]
                    key.insert(axis, v)
                    return tuple(key)
                low, mid, high = f[at(-1)], f[at(0)], f[at(1)]
                both = high + low
                g[at(-1)] = both + mid
                g[at(0)] = high - low
                g[at(1)] = both
        f = g
    m = {(p, q, r): f[p - 1, q - 1, r - 1] for p in range(3) for q in range(3) for r in range(3)}
    rho, jx, jy, jz = m[0, 0, 0], m[1, 0, 0], m[0, 1, 0], m[0, 0, 1]
    force = BUOYANCY * (heat - REFERENCE_HEAT)
    flow_z = jz + 0.5 * force
    inverse = 1.0 / rho
    ux, uy, uz = jx * inverse, jy * inverse, flow_z * inverse
    third = rho * (1.0 / 3.0)
    xx, yy, zz = jx * ux, jy * uy, flow_z * uz
    square = {0: xx, 1: yy, 2: zz}
    flux = {0: jx, 1: jy, 2: flow_z}
    cross = {(0, 1): jx * uy, (0, 2): jx * uz, (1, 2): jy * uz}
    out = {}
    for k in RELAXED:
        odd = tuple(n for n in range(3) if k[n] == 1)
        if len(odd) == 3:
            out[k] = m[k] * coef(k, "keep")
            continue
        if len(odd) == 0:
            base = third
            for n in range(3):
                if k[n] == 2:
                    base = base + square[n]
        elif len(odd) == 1:
            base = flux[odd[0]]
        else:
            base = cross[odd]
        out[k] = m[k] * coef(k, "keep") + base * coef(k, "gain")
    out[0, 0, 0] = rho
    out[1, 0, 0] = 0.5 * jx
    out[0, 1, 0] = 0.5 * jy
    out[0, 0, 1] = 0.5 * (jz + force)
    f = {tuple(v - 1 for v in k): out[k] for k in out}
    for axis in range(3):
        g = {}
        for one in (-1, 0, 1):
            for two in (-1, 0, 1):
                def at(v):
                    key = [one, two]
                    key.insert(axis, v)
                    return tuple(key)
                zero, first, second = f[at(-1)], f[at(0)], f[at(1)]
                half = 0.5 * second
                g[at(-1)] = half - first
                g[at(0)] = zero - second
                g[at(1)] = half + first
        f = g
    return f, (inverse, jx, jy, jz)


def collide_heat(g, speed, omega):
    total = g[0]
    for k in range(1, 7):
        total = total + g[k]
    keep = 1.0 - omega
    part = omega * total * 0.125
    four = 4.0 * part
    out = [keep * g[0] + 2.0 * part]
    for d in range(3):
        push = four * speed[d]
        out.append(keep * g[1 + 2 * d] + (part + push))
        out.append(keep * g[2 + 2 * d] + (part - push))
    return out


def sum_heat(g):
    total = g[0]
    for k in range(1, 7):
        total = total + g[k]
    return total


def kernel(sizes, pop_ref, th_ref, vel_ref, solid_ref, ph_ref, cond_ref, rates_ref, fout, tout, post, stage, aux, coefs, hro, hrx, ar, ari, aps, apr, zs, zr, gs,
           send_sem, recv_sem, a_send, a_recv, z_send, z_recv, t_send, t_recv):
    me = {n: lax.axis_index(n) for n in sizes}
    names = list(sizes)

    def device(offset):
        return tuple(lax.rem(me[n] + (k + sizes[n]), sizes[n]) if k else me[n] for n, k in zip(names, offset))

    mine = me["grp"]
    barrier = pltpu.get_barrier_semaphore()
    others = [(0, a, b) for a in (-1, 0, 1) for b in (-1, 0, 1) if (a, b) != (0, 0)] + [(d, 0, 0) for d in (1, 2, 3)]
    for offset in others:
        pl.semaphore_signal(barrier, inc=1, device_id=device(offset), device_id_type=MESH)
    pl.semaphore_wait(barrier, len(others))

    lane = lax.broadcasted_iota(jnp.int32, (8, 128), 1)
    unit = (lane + 16) % 32

    def chunk(j):
        return pl.ds(pl.multiple_of(j * 128, 128), 128)

    a_copies = []
    for d in (2, 1, 3):
        target = lax.rem(mine + d, 4)
        to = device((d, 0, 0))
        for n, (src, dst) in enumerate(((th_ref.at[:, 0, :, chunk(target)], ar.at[mine]), (ph_ref.at[0, :, chunk(target)], ari.at[mine]))):
            a_copies.append(pltpu.make_async_remote_copy(src_ref=src, dst_ref=dst, send_sem=a_send.at[n, d - 1], recv_sem=a_recv.at[n, d - 1], device_id=to, device_id_type=MESH))
            a_copies[-1].start()
    for m in range(4):
        left, right = slice(128 * ((m + 3) % 4), 128 * ((m + 3) % 4) + 128), slice(128 * ((m + 1) % 4), 128 * ((m + 1) % 4) + 128)
        pack = None
        for k in range(8):
            if k < 7:
                both = jnp.where(lane < 64, th_ref[k, 0, :, right], th_ref[k, 0, :, left])
            else:
                both = jnp.where(lane < 64, ph_ref[0, :, right], ph_ref[0, :, left]).astype(F32)
            both = turn(both, 16 * k + 8)
            pack = both if pack is None else jnp.where(lane // 16 == k, both, pack)
        aps[m] = pack
    for d in (2, 1, 3):
        target = lax.rem(mine + d, 4)
        a_copies.append(pltpu.make_async_remote_copy(src_ref=aps.at[target], dst_ref=apr.at[mine], send_sem=a_send.at[2, d - 1], recv_sem=a_recv.at[2, d - 1], device_id=device((d, 0, 0)), device_id_type=MESH))
        a_copies[-1].start()
    apr[mine] = aps[mine]
    ar[mine] = th_ref[:, 0, :, chunk(mine)]
    ari[mine] = ph_ref[0, :, chunk(mine)]

    group = [(unit == unit) & (((lane - center(p) + 16) % 128) < 32) for p in range(4)]
    solid = [turn(solid_ref[p], center(p)) != 0 for p in range(4)]
    fields = [("f", key) for key in FLOW] + [("u", n) for n in range(3)]

    def merged(field):
        kind, key = field
        tile = None
        for p in range(4):
            if kind == "f":
                value = turn(pop_ref[FLOW.index(key), p], center(p))
                value = jnp.where(solid[p], jnp.nan, value)
                stage[FLOW_AT[key], p] = value
            else:
                value = turn(vel_ref[key, p], center(p))
                aux[1 + key, p] = value
            tile = value if tile is None else jnp.where(group[p], value, tile)
        return tile

    z_copies = []
    for n in range(15):
        one, two = merged(fields[2 * n]), merged(fields[2 * n + 1])
        zs[n] = jnp.where((unit >= 8) & (unit < 24), one, turn(two, 16))
        if n % 5 == 4:
            for side, d in ((0, 1), (1, -1)):
                z_copies.append(pltpu.make_async_remote_copy(src_ref=zs.at[n - 4 : n + 1], dst_ref=zr.at[side, n - 4 : n + 1], send_sem=z_send.at[side, n // 5], recv_sem=z_recv.at[side, n // 5], device_id=device((d, 0, 0)), device_id_type=MESH))
                z_copies[-1].start()

    for k in RELAXED:
        rate = rates_ref[9 * k[0] + 3 * k[1] + k[2]]
        half = 0.5 ** sum(v == 1 for v in k)
        coefs[COEF[k, "keep"]] = jnp.full((8, 128), (1.0 - rate) * half, F32)
        if (k, "gain") in COEF:
            coefs[COEF[k, "gain"]] = jnp.full((8, 128), rate * (half * gain_scale(k)), F32)

    def coef(k, kind):
        return coefs[COEF[k, kind]]

    for copy in a_copies:
        copy.wait()

    def omega_of(ids):
        level = jnp.full((8, 128), cond_ref[3], F32)
        for n in range(3):
            level = jnp.where(ids == n, cond_ref[n], level)
        return 1.0 / (0.5 + 4.0 * level)

    for p in range(4):
        g = [turn(ar[p, k], center(p)) for k in range(7)]
        for k in range(7):
            stage[HEAT_AT[k], p] = g[k]
        aux[0, p] = sum_heat(g)
        aux[4, p] = omega_of(turn(ari[p], center(p)))
    tiles = []
    for k in range(8):
        tile = None
        for p in range(4):
            value = turn(apr[p], center(p) - 16 * k - 8)
            tile = value if tile is None else jnp.where(group[p], value, tile)
        tiles.append(tile)
    for k in range(7):
        stage[HEAT_AT[k], 4] = tiles[k]
    aux[0, 4] = sum_heat(tiles[:7])
    aux[4, 4] = omega_of(tiles[7])

    for copy in z_copies:
        copy.wait()
    from_left = (unit // 8) % 2 == 1
    for n in range(15):
        both = jnp.where(from_left, zr[0, n], zr[1, n])
        for field, value in ((fields[2 * n], both), (fields[2 * n + 1], turn(both, -16))):
            kind, key = field
            if kind == "f":
                stage[FLOW_AT[key], 4] = value
            else:
                aux[1 + key, 4] = value

    def round_copies(parity):
        out = []
        for n, (offset, span, s_slots, t_slots, s_rows, t_rows) in enumerate(MESSAGES):
            out.append(pltpu.make_async_remote_copy(
                src_ref=post.at[parity, span[0] : span[1], s_slots[0] : s_slots[1], s_rows[0] : s_rows[1]],
                dst_ref=post.at[parity, span[0] : span[1], t_slots[0] : t_slots[1], t_rows[0] : t_rows[1]],
                send_sem=send_sem.at[parity, n], recv_sem=recv_sem.at[parity, n], device_id=device(offset), device_id_type=MESH))
        return out

    def own_slot(q, s):
        return H_SLOT if s == 4 else slot_of(VELOCITY[q][0], s)

    def put(parity, s, flow, heat):
        for key in FLOW:
            q = FLOW_AT[key]
            post[parity, q, own_slot(q, s), ROW : ROW + 8] = flow[key]
        for k in range(7):
            q = HEAT_AT[k]
            post[parity, q, own_slot(q, s), ROW : ROW + 8] = heat[k]

    def window(b):
        return slice(ROW - b, ROW - b + 8)

    def arrive(parity, q, s):
        a, b, c = VELOCITY[q]
        rows = window(b)
        amount = 32 * a + c
        if s < 4:
            base = turn(post[parity, q, slot_of(a, s - a), rows], amount)
            if c:
                halo = hro if 0 <= s - a < PLANES else hrx
                spot = center(s) if c == 1 else (center(s) - 1) % 128
                base = jnp.where(lane == spot, halo[q], base)
            return base
        base = post[parity, q, H_SLOT, rows]
        if a:
            outer = center(-1) if a == 1 else center(4)
            base = jnp.where((lane - outer + 16) % 128 < 32, post[parity, q, XH_SLOT, rows], base)
        if c:
            for p in range(4):
                spot = (center(p - a) - 1) % 128 if c == 1 else center(p - a)
                base = jnp.where(lane == spot, post[parity, q, slot_of(a, p - a), rows], base)
        return turn(base, amount)

    def flow_arrivals(parity, s):
        f = {}
        for key in FLOW:
            q = FLOW_AT[key]
            if key == (0, 0, 0):
                f[key] = post[parity, q, own_slot(q, s), ROW : ROW + 8]
                continue
            back = FLOW_AT[tuple(-v for v in key)]
            value = arrive(parity, q, s)
            f[key] = jnp.where(value != value, post[parity, back, own_slot(back, s), ROW : ROW + 8], value)
        return f

    def halo_rolls(parity, inner):
        for q in range(COUNT):
            a, b, c = VELOCITY[q]
            if c and inner:
                hro[q] = turn(post[parity, q, H_SLOT, window(b)], 32 * a + c)
            elif c and a:
                hrx[q] = turn(post[parity, q, XH_SLOT, window(b)], 32 * a + c)

    def start(parity, s, f, g, turned):
        heat_sum = sum_heat(g)
        old = aux[0, s]
        heat = old if turned is None else jnp.where(turned, heat_sum, old)
        flow, (inverse, jx, jy, jz) = collide_flow(f, heat, coef)
        speed = [aux[1 + n, s] for n in range(3)]
        if turned is not None:
            jz = jz + (0.5 * BUOYANCY) * (old - REFERENCE_HEAT)
            fresh = [j * inverse for j in (jx, jy, jz)]
            fresh = [jnp.where(v == v, v, 0.0) for v in fresh]
            speed = [jnp.where(turned, fresh[n], speed[n]) for n in range(3)]
            aux[0, s] = heat
            for n in range(3):
                aux[1 + n, s] = speed[n]
        put(parity, s, flow, collide_heat(g, speed, aux[4, s]))

    for s in (0, 3, 4, 1, 2):
        start(0, s, {key: stage[FLOW_AT[key], s] for key in FLOW}, [stage[HEAT_AT[k], s] for k in range(7)], None)
    for copy in round_copies(0):
        copy.start()

    def advance(step, carry):
        before = lax.rem(step + 1, 2)
        after = lax.rem(step, 2)
        turned = jnp.broadcast_to(step == STEPS, (8, 128))
        copies = round_copies(before)

        def pair(s):
            start(after, s, flow_arrivals(before, s), [arrive(before, HEAT_AT[k], s) for k in range(7)], turned)

        for copy in copies[FIRST_Y:]:
            copy.wait()
        halo_rolls(before, True)
        pair(1)
        pair(2)
        for copy in copies[:FIRST_Y]:
            copy.wait()
        halo_rolls(before, False)
        for s in (0, 3, 4):
            pair(s)
        for copy in round_copies(after):
            copy.start()
        return carry

    total = STEPS * WINDOWS
    lax.fori_loop(1, total, advance, 0)

    last = (total - 1) % 2
    copies = round_copies(last)
    for copy in copies:
        copy.wait()
    halo_rolls(last, True)
    halo_rolls(last, False)
    for p in range(4):
        for k in range(7):
            gs[p, k] = turn(arrive(last, HEAT_AT[k], p), -center(p))
    t_copies = []
    for d in (2, 1, 3):
        target = lax.rem(mine + d, 4)
        t_copies.append(pltpu.make_async_remote_copy(src_ref=gs.at[target], dst_ref=tout.at[:, 0, :, chunk(mine)], send_sem=t_send.at[d - 1], recv_sem=t_recv.at[d - 1], device_id=device((d, 0, 0)), device_id_type=MESH))
        t_copies[-1].start()
    tout[:, 0, :, chunk(mine)] = gs[mine]
    for p in range(4):
        f = flow_arrivals(last, p)
        for n, key in enumerate(FLOW):
            fout[n, p] = jnp.where(solid_ref[p] != 0, pop_ref[n, p], turn(f[key], -center(p)))
    for copy in t_copies:
        copy.wait()


def solution(mesh):
    sizes = dict(mesh.shape)

    def on_device(populations, thermal, velocity_prev, solid, phase_ids, conductivity, rates):
        vmem = pl.BlockSpec(memory_space=pltpu.VMEM)
        smem = pl.BlockSpec(memory_space=pltpu.SMEM)
        tile = (8, 128)
        return pl.pallas_call(
            functools.partial(kernel, sizes),
            out_shape=(jax.ShapeDtypeStruct(populations.shape, F32), jax.ShapeDtypeStruct(thermal.shape, F32)),
            in_specs=[vmem] * 5 + [smem] * 2,
            out_specs=(vmem, vmem),
            scratch_shapes=[
                pltpu.VMEM((2, COUNT, 7, 24, 128), F32),
                pltpu.VMEM((COUNT, 5) + tile, F32),
                pltpu.VMEM((5, 5) + tile, F32),
                pltpu.VMEM((len(COEF),) + tile, F32),
                pltpu.VMEM((COUNT,) + tile, F32),
                pltpu.VMEM((COUNT,) + tile, F32),
                pltpu.VMEM((4, 7) + tile, F32),
                pltpu.VMEM((4,) + tile, jnp.int32),
                pltpu.VMEM((4,) + tile, F32),
                pltpu.VMEM((4,) + tile, F32),
                pltpu.VMEM((15,) + tile, F32),
                pltpu.VMEM((2, 15) + tile, F32),
                pltpu.VMEM((4, 7) + tile, F32),
                pltpu.SemaphoreType.DMA((2, len(MESSAGES))),
                pltpu.SemaphoreType.DMA((2, len(MESSAGES))),
                pltpu.SemaphoreType.DMA((3, 3)),
                pltpu.SemaphoreType.DMA((3, 3)),
                pltpu.SemaphoreType.DMA((2, 3)),
                pltpu.SemaphoreType.DMA((2, 3)),
                pltpu.SemaphoreType.DMA((3,)),
                pltpu.SemaphoreType.DMA((3,)),
            ],
            compiler_params=pltpu.CompilerParams(collective_id=0, has_side_effects=True, vmem_limit_bytes=48 * 1024 * 1024),
        )(populations, thermal, velocity_prev, solid, phase_ids, conductivity, rates)

    in_specs = (
        P(None, "gx", "gy", "grp"),
        P(None, ("gx", "grp"), "gy", None),
        P(None, "gx", "gy", "grp"),
        P("gx", "gy", "grp"),
        P(("gx", "grp"), "gy", None),
        P(),
        P(),
    )
    out_specs = (P(None, "gx", "gy", "grp"), P(None, ("gx", "grp"), "gy", None))
    return jax.shard_map(on_device, mesh=mesh, in_specs=in_specs, out_specs=out_specs, check_vma=False)
```

time: 334 us -> 67.6 us (0.20)
  the two profiles are of different devices: /device:TPU:25 before, /device:TPU:1 now
where the time goes in v1:
time: 67.6 us; the launch traced here: 67.3 us
  Pallas kernels  59.8 us (88%)
  local copies, waits for them, and re-layouts  6.86 us (10%)
    pallas_call x1, Pallas kernels, on_device(): pl.pallas_call(functools.partial(kernel, sizes), out_shape=(jax.ShapeDtyp...  59.8 us
    unnamed x16, local copies, waits for them, and re-layouts  6.86 us

profile of v1, /device:TPU:1, one launch (start us, length us, event | category | flops | bytes accessed | tf_op | source)
XLA Modules:
  0.0 67.3 jit_solution(5650234721725456143)
XLA Ops:
  0.6 0.0 copy-start
  0.6 1.0 %copy-done = f32[27,4,8,128]{3,2,1,0:T(8,128)S(1)} copy-done((f32[27,4,8,128]{3,2,1,0:T(8,128)S(1)}, f32[27,4,8,128]{3,2,1,0:T(8,128)}, u32[]{:S(2)}) %copy-start) | copy-done | bytes 442392
  1.6 0.0 copy-start.1
  1.6 0.9 %copy-done.1 = f32[7,1,8,512]{3,2,1,0:T(8,128)S(1)} copy-done((f32[7,1,8,512]{3,2,1,0:T(8,128)S(1)}, f32[7,1,8,512]{3,2,1,0:T(8,128)}, u32[]{:S(2)}) %copy-start.1) | copy-done | bytes 114712
  2.5 0.0 copy-start.2
  2.5 0.8 %copy-done.2 = f32[3,4,8,128]{3,2,1,0:T(8,128)S(1)} copy-done((f32[3,4,8,128]{3,2,1,0:T(8,128)S(1)}, f32[3,4,8,128]{3,2,1,0:T(8,128)}, u32[]{:S(2)}) %copy-start.2) | copy-done | bytes 49176
  3.3 0.0 copy-start.3
  3.3 0.7 %copy-done.3 = s32[4,8,128]{2,1,0:T(8,128)S(1)} copy-done((s32[4,8,128]{2,1,0:T(8,128)S(1)}, s32[4,8,128]{2,1,0:T(8,128)}, u32[]{:S(2)}) %copy-start.3) | copy-done | bytes 16408
  4.1 0.0 copy-start.4
  4.1 0.7 %copy-done.4 = s32[1,8,512]{2,1,0:T(8,128)S(1)} copy-done((s32[1,8,512]{2,1,0:T(8,128)S(1)}, s32[1,8,512]{2,1,0:T(8,128)}, u32[]{:S(2)}) %copy-start.4) | copy-done | bytes 16408
  4.8 0.0 copy-start.5
  4.8 0.7 copy-done.5
  5.4 0.0 copy-start.6
  5.4 0.7 copy-done.6
  6.1 59.8 %shard_map.86 = (f32[27,4,8,128]{3,2,1,0:T(8,128)S(1)}, f32[7,1,8,512]{3,2,1,0:T(8,128)S(1)}) custom-call(f32[27,4,8,128]{3,2,1,0:T(8,128)S(1)} %copy-done, f32[7,1,8,512]{3,2,1,0:T(8,128)S(1)} %copy-done.1, f32[3,4,8,128]{3,2,1,0:T(8,128)S(1)} %copy-done.2, s32[4,8,128]{2,1,0:T(8,128)S(1)} %copy-done.3, s32[1,8,512]{2,1,0:T(8,128)S(1)} %copy-done.4, ...), custom_call_target="tpu_custom_call" | custom-call | tf_op jit(solution)/shard_map/pallas_call | solution.py:435
  65.9 0.8 %copy.11 = f32[27,4,8,128]{3,2,1,0:T(8,128)} copy(f32[27,4,8,128]{3,2,1,0:T(8,128)S(1)} %get-tuple-element.4) | data formatting | bytes 884736
  66.6 0.6 copy.12
Async XLA Ops:
  0.6 1.0 %copy-start = (f32[27,4,8,128]{3,2,1,0:T(8,128)S(1)}, f32[27,4,8,128]{3,2,1,0:T(8,128)}, u32[]{:S(2)}) copy-start(f32[27,4,8,128]{3,2,1,0:T(8,128)} %pop_ref.1) | copy-start | bytes 1327108
  1.6 0.9 %copy-start.1 = (f32[7,1,8,512]{3,2,1,0:T(8,128)S(1)}, f32[7,1,8,512]{3,2,1,0:T(8,128)}, u32[]{:S(2)}) copy-start(f32[7,1,8,512]{3,2,1,0:T(8,128)} %th_ref.1) | copy-start | bytes 344068
  2.5 0.8 %copy-start.2 = (f32[3,4,8,128]{3,2,1,0:T(8,128)S(1)}, f32[3,4,8,128]{3,2,1,0:T(8,128)}, u32[]{:S(2)}) copy-start(f32[3,4,8,128]{3,2,1,0:T(8,128)} %vel_ref.1) | copy-start | bytes 147460
  3.3 0.7 %copy-start.3 = (s32[4,8,128]{2,1,0:T(8,128)S(1)}, s32[4,8,128]{2,1,0:T(8,128)}, u32[]{:S(2)}) copy-start(s32[4,8,128]{2,1,0:T(8,128)} %solid_ref.1) | copy-start | bytes 49156
  4.1 0.7 %copy-start.4 = (s32[1,8,512]{2,1,0:T(8,128)S(1)}, s32[1,8,512]{2,1,0:T(8,128)}, u32[]{:S(2)}) copy-start(s32[1,8,512]{2,1,0:T(8,128)} %ph_ref.1) | copy-start | bytes 49156
  4.8 0.7 copy-start.5
  5.4 0.7 copy-start.6

commit v2 on v1

--- a/solution.py
+++ b/solution.py
@@ -17,6 +17,7 @@
 
 RING = [(-1, -1), (-1, 0), "x-", (-1, 1), (0, 1), "y+", (1, 1), (1, 0), "x+", (1, -1), (0, -1), "y-", (0, 0), "0", "z+", "z-"]
 THERMAL = {"0": (0, 0, 0), "x+": (1, 0, 0), "x-": (-1, 0, 0), "y+": (0, 1, 0), "y-": (0, -1, 0), "z+": (0, 0, 1), "z-": (0, 0, -1)}
+HOME_ORDER = [0, 5, 6, 3, 4, 1, 2]
 HEAT_ORDER = ["0", "x+", "x-", "y+", "y-", "z+", "z-"]
 VELOCITY = []
 FLOW_AT = {}
@@ -168,8 +169,13 @@
     return total
 
 
-def kernel(sizes, pop_ref, th_ref, vel_ref, solid_ref, ph_ref, cond_ref, rates_ref, fout, tout, post, stage, aux, coefs, hro, hrx, ar, ari, aps, apr, zs, zr, gs,
-           send_sem, recv_sem, a_send, a_recv, z_send, z_recv, t_send, t_recv):
+def kernel(sizes, pop_in, th_in, vel_in, solid_in, ph_in, cond_in, rates_in, fout, tout, pop_ref, th_ref, vel_ref, solid_ref, ph_ref, cond_ref, rates_ref,
+           post, stage, aux, coefs, hro, hrx, ar, ari, aps, apr, zs, zr, gs, own, own_row,
+           in_sem, send_sem, recv_sem, a_send, a_recv, z_send, z_recv, t_send, t_recv):
+    loads = [pltpu.make_async_copy(src, dst, in_sem.at[n]) for n, (src, dst) in enumerate((
+        (th_in, th_ref), (ph_in, ph_ref), (pop_in, pop_ref), (solid_in, solid_ref), (vel_in, vel_ref), (rates_in, rates_ref), (cond_in, cond_ref)))]
+    for copy in loads:
+        copy.start()
     me = {n: lax.axis_index(n) for n in sizes}
     names = list(sizes)
 
@@ -181,7 +187,6 @@
     others = [(0, a, b) for a in (-1, 0, 1) for b in (-1, 0, 1) if (a, b) != (0, 0)] + [(d, 0, 0) for d in (1, 2, 3)]
     for offset in others:
         pl.semaphore_signal(barrier, inc=1, device_id=device(offset), device_id_type=MESH)
-    pl.semaphore_wait(barrier, len(others))
 
     lane = lax.broadcasted_iota(jnp.int32, (8, 128), 1)
     unit = (lane + 16) % 32
@@ -189,13 +194,8 @@
     def chunk(j):
         return pl.ds(pl.multiple_of(j * 128, 128), 128)
 
-    a_copies = []
-    for d in (2, 1, 3):
-        target = lax.rem(mine + d, 4)
-        to = device((d, 0, 0))
-        for n, (src, dst) in enumerate(((th_ref.at[:, 0, :, chunk(target)], ar.at[mine]), (ph_ref.at[0, :, chunk(target)], ari.at[mine]))):
-            a_copies.append(pltpu.make_async_remote_copy(src_ref=src, dst_ref=dst, send_sem=a_send.at[n, d - 1], recv_sem=a_recv.at[n, d - 1], device_id=to, device_id_type=MESH))
-            a_copies[-1].start()
+    loads[0].wait()
+    loads[1].wait()
     for m in range(4):
         left, right = slice(128 * ((m + 3) % 4), 128 * ((m + 3) % 4) + 128), slice(128 * ((m + 1) % 4), 128 * ((m + 1) % 4) + 128)
         pack = None
@@ -207,15 +207,21 @@
             both = turn(both, 16 * k + 8)
             pack = both if pack is None else jnp.where(lane // 16 == k, both, pack)
         aps[m] = pack
-    for d in (2, 1, 3):
-        target = lax.rem(mine + d, 4)
-        a_copies.append(pltpu.make_async_remote_copy(src_ref=aps.at[target], dst_ref=apr.at[mine], send_sem=a_send.at[2, d - 1], recv_sem=a_recv.at[2, d - 1], device_id=device((d, 0, 0)), device_id_type=MESH))
-        a_copies[-1].start()
     apr[mine] = aps[mine]
     ar[mine] = th_ref[:, 0, :, chunk(mine)]
     ari[mine] = ph_ref[0, :, chunk(mine)]
+    pl.semaphore_wait(barrier, len(others))
+    a_copies = []
+    for d in (2, 1, 3):
+        target = lax.rem(mine + d, 4)
+        to = device((d, 0, 0))
+        for n, (src, dst) in enumerate(((th_ref.at[:, 0, :, chunk(target)], ar.at[mine]), (ph_ref.at[0, :, chunk(target)], ari.at[mine]), (aps.at[target], apr.at[mine]))):
+            a_copies.append(pltpu.make_async_remote_copy(src_ref=src, dst_ref=dst, send_sem=a_send.at[n, d - 1], recv_sem=a_recv.at[n, d - 1], device_id=to, device_id_type=MESH))
+            a_copies[-1].start()
 
     group = [(unit == unit) & (((lane - center(p) + 16) % 128) < 32) for p in range(4)]
+    for copy in loads[2:5]:
+        copy.wait()
     solid = [turn(solid_ref[p], center(p)) != 0 for p in range(4)]
     fields = [("f", key) for key in FLOW] + [("u", n) for n in range(3)]
 
@@ -234,14 +240,21 @@
         return tile
 
     z_copies = []
-    for n in range(15):
-        one, two = merged(fields[2 * n]), merged(fields[2 * n + 1])
-        zs[n] = jnp.where((unit >= 8) & (unit < 24), one, turn(two, 16))
-        if n % 5 == 4:
+    for n in range(8):
+        low, high = None, None
+        for k, field in enumerate(fields[4 * n : 4 * n + 4]):
+            value = turn(merged(field), 8 * k - 8)
+            low = value if low is None else jnp.where(unit // 8 == k, value, low)
+            high = value if high is None else jnp.where(unit // 8 == (k + 1) % 4, value, high)
+        zs[0, n] = low
+        zs[1, n] = high
+        if n % 4 == 3:
             for side, d in ((0, 1), (1, -1)):
-                z_copies.append(pltpu.make_async_remote_copy(src_ref=zs.at[n - 4 : n + 1], dst_ref=zr.at[side, n - 4 : n + 1], send_sem=z_send.at[side, n // 5], recv_sem=z_recv.at[side, n // 5], device_id=device((d, 0, 0)), device_id_type=MESH))
+                z_copies.append(pltpu.make_async_remote_copy(src_ref=zs.at[side, n - 3 : n + 1], dst_ref=zr.at[side, n - 3 : n + 1], send_sem=z_send.at[side, n // 4], recv_sem=z_recv.at[side, n // 4], device_id=device((d, 0, 0)), device_id_type=MESH))
                 z_copies[-1].start()
 
+    loads[5].wait()
+    loads[6].wait()
     for k in RELAXED:
         rate = rates_ref[9 * k[0] + 3 * k[1] + k[2]]
         half = 0.5 ** sum(v == 1 for v in k)
@@ -281,11 +294,10 @@
 
     for copy in z_copies:
         copy.wait()
-    from_left = (unit // 8) % 2 == 1
-    for n in range(15):
-        both = jnp.where(from_left, zr[0, n], zr[1, n])
-        for field, value in ((fields[2 * n], both), (fields[2 * n + 1], turn(both, -16))):
-            kind, key = field
+    for n in range(8):
+        low, high = zr[0, n], zr[1, n]
+        for k, (kind, key) in enumerate(fields[4 * n : 4 * n + 4]):
+            value = turn(jnp.where(unit // 8 == k, low, high), 8 - 8 * k)
             if kind == "f":
                 stage[FLOW_AT[key], 4] = value
             else:
@@ -376,6 +388,51 @@
     for copy in round_copies(0):
         copy.start()
 
+    total = STEPS * WINDOWS
+
+    def home_copy(src, dst, n, d, to):
+        return pltpu.make_async_remote_copy(src_ref=src, dst_ref=dst, send_sem=t_send.at[n, d], recv_sem=t_recv.at[n, d], device_id=to, device_id_type=MESH)
+
+    def moved(n, by):
+        return lax.rem(me[n] + by, sizes[n])
+
+    def home_copies():
+        out = []
+        for d in (2, 3, 1, 0):
+            j = lax.rem(mine + d, 4)
+            up = moved("gx", jnp.where(j == 0, 1, 0))
+            down = moved("gx", jnp.where(j == 3, sizes["gx"] - 1, 0))
+            out.append((home_copy(gs.at[lax.rem(j + 3, 4), 5], own.at[mine, 5], 1, d, (j, up, me["gy"])), mine == 0 if d == 0 else None))
+            out.append((home_copy(gs.at[lax.rem(j + 1, 4), 6], own.at[mine, 6], 2, d, (j, down, me["gy"])), mine == 3 if d == 0 else None))
+            if d:
+                out.append((home_copy(gs.at[j, 0:5], own.at[mine, 0:5], 0, d, (j, me["gx"], me["gy"])), None))
+            out.append((home_copy(gs.at[j, 3, 7:8], own_row.at[mine, 0, 7:8], 3, d, (j, me["gx"], moved("gy", 1))), None))
+            out.append((home_copy(gs.at[j, 4, 0:1], own_row.at[mine, 1, 0:1], 4, d, (j, me["gx"], moved("gy", sizes["gy"] - 1))), None))
+        return out
+
+    def perform(copies, what):
+        for copy, only in copies:
+            if only is None:
+                what(copy)
+            else:
+                pl.when(only)(functools.partial(what, copy))
+
+    def home_start(parity):
+        for p in range(4):
+            for n, k in enumerate(HOME_ORDER):
+                q = HEAT_AT[k]
+                gs[p, n] = turn(post[parity, q, own_slot(q, p), ROW : ROW + 8], -center(p))
+        perform(home_copies(), lambda copy: copy.start())
+        own[mine, 0:5] = gs[mine, 0:5]
+
+        @pl.when(mine != 0)
+        def _():
+            own[mine, 5] = gs[lax.rem(mine + 3, 4), 5]
+
+        @pl.when(mine != 3)
+        def _():
+            own[mine, 6] = gs[lax.rem(mine + 1, 4), 6]
+
     def advance(step, carry):
         before = lax.rem(step + 1, 2)
         after = lax.rem(step, 2)
@@ -395,11 +452,15 @@
         halo_rolls(before, False)
         for s in (0, 3, 4):
             pair(s)
+
+        @pl.when(step == total - 1)
+        def _():
+            home_start(after)
+
         for copy in round_copies(after):
             copy.start()
         return carry
 
-    total = STEPS * WINDOWS
     lax.fori_loop(1, total, advance, 0)
 
     last = (total - 1) % 2
@@ -409,20 +470,19 @@
     halo_rolls(last, True)
     halo_rolls(last, False)
     for p in range(4):
-        for k in range(7):
-            gs[p, k] = turn(arrive(last, HEAT_AT[k], p), -center(p))
-    t_copies = []
-    for d in (2, 1, 3):
-        target = lax.rem(mine + d, 4)
-        t_copies.append(pltpu.make_async_remote_copy(src_ref=gs.at[target], dst_ref=tout.at[:, 0, :, chunk(mine)], send_sem=t_send.at[d - 1], recv_sem=t_recv.at[d - 1], device_id=device((d, 0, 0)), device_id_type=MESH))
-        t_copies[-1].start()
-    tout[:, 0, :, chunk(mine)] = gs[mine]
-    for p in range(4):
         f = flow_arrivals(last, p)
         for n, key in enumerate(FLOW):
             fout[n, p] = jnp.where(solid_ref[p] != 0, pop_ref[n, p], turn(f[key], -center(p)))
-    for copy in t_copies:
-        copy.wait()
+    perform(home_copies(), lambda copy: copy.wait())
+    row = lax.broadcasted_iota(jnp.int32, (8, 128), 0)
+    for n in range(4):
+        tiles = {k: own[n, place] for place, k in enumerate(HOME_ORDER)}
+        tiles[3] = pltpu.roll(jnp.where(row == 7, own_row[n, 0], tiles[3]), 1, 0)
+        tiles[4] = pltpu.roll(jnp.where(row == 0, own_row[n, 1], tiles[4]), 7, 0)
+        tiles[5] = turn(jnp.where(lane == 127, own[(n + 3) % 4, HOME_ORDER.index(5)], tiles[5]), 1)
+        tiles[6] = turn(jnp.where(lane == 0, own[(n + 1) % 4, HOME_ORDER.index(6)], tiles[6]), -1)
+        for k in range(7):
+            tout[k, 0, :, 128 * n : 128 * n + 128] = tiles[k]
 
 
 def solution(mesh):
@@ -430,14 +490,16 @@
 
     def on_device(populations, thermal, velocity_prev, solid, phase_ids, conductivity, rates):
         vmem = pl.BlockSpec(memory_space=pltpu.VMEM)
-        smem = pl.BlockSpec(memory_space=pltpu.SMEM)
+        hbm = pl.BlockSpec(memory_space=pltpu.HBM)
         tile = (8, 128)
         return pl.pallas_call(
             functools.partial(kernel, sizes),
             out_shape=(jax.ShapeDtypeStruct(populations.shape, F32), jax.ShapeDtypeStruct(thermal.shape, F32)),
-            in_specs=[vmem] * 5 + [smem] * 2,
+            in_specs=[hbm] * 7,
             out_specs=(vmem, vmem),
-            scratch_shapes=[
+            scratch_shapes=[pltpu.VMEM(v.shape, v.dtype) for v in (populations, thermal, velocity_prev, solid, phase_ids)]
+            + [pltpu.SMEM(v.shape, v.dtype) for v in (conductivity, rates)]
+            + [
                 pltpu.VMEM((2, COUNT, 7, 24, 128), F32),
                 pltpu.VMEM((COUNT, 5) + tile, F32),
                 pltpu.VMEM((5, 5) + tile, F32),
@@ -448,20 +510,23 @@
                 pltpu.VMEM((4,) + tile, jnp.int32),
                 pltpu.VMEM((4,) + tile, F32),
                 pltpu.VMEM((4,) + tile, F32),
-                pltpu.VMEM((15,) + tile, F32),
-                pltpu.VMEM((2, 15) + tile, F32),
+                pltpu.VMEM((2, 8) + tile, F32),
+                pltpu.VMEM((2, 8) + tile, F32),
                 pltpu.VMEM((4, 7) + tile, F32),
+                pltpu.VMEM((4, 7) + tile, F32),
+                pltpu.VMEM((4, 2) + tile, F32),
+                pltpu.SemaphoreType.DMA((7,)),
                 pltpu.SemaphoreType.DMA((2, len(MESSAGES))),
                 pltpu.SemaphoreType.DMA((2, len(MESSAGES))),
                 pltpu.SemaphoreType.DMA((3, 3)),
                 pltpu.SemaphoreType.DMA((3, 3)),
-                pltpu.SemaphoreType.DMA((2, 3)),
-                pltpu.SemaphoreType.DMA((2, 3)),
-                pltpu.SemaphoreType.DMA((3,)),
-                pltpu.SemaphoreType.DMA((3,)),
+                pltpu.SemaphoreType.DMA((2, 2)),
+                pltpu.SemaphoreType.DMA((2, 2)),
+                pltpu.SemaphoreType.DMA((5, 4)),
+                pltpu.SemaphoreType.DMA((5, 4)),
             ],
             compiler_params=pltpu.CompilerParams(collective_id=0, has_side_effects=True, vmem_limit_bytes=48 * 1024 * 1024),
-        )(populations, thermal, velocity_prev, solid, phase_ids, conductivity, rates)
+        )(*[pltpu.with_memory_space_constraint(v, pltpu.HBM) for v in (populations, thermal, velocity_prev, solid, phase_ids, conductivity, rates)])
 
     in_specs = (
         P(None, "gx", "gy", "grp"),

time: 67.6 us -> 57.6 us (0.85)
  local copies, waits for them, and re-layouts: 6.86 us -> 1.41 us
  Pallas kernels: 59.8 us -> 55.1 us
    unnamed x16 -> x2, local copies, waits for them, and re-layouts: 6.86 us -> 1.41 us
    pallas_call x1, Pallas kernels: 59.8 us -> 55.1 us  [on_device(): pl.pallas_call(functools.partial(kernel, sizes), out_shape=(jax.ShapeDtyp...]
where the time goes in v2:
time: 57.6 us; the launch traced here: 57.1 us
  Pallas kernels  55.1 us (96%)
  local copies, waits for them, and re-layouts  1.41 us (2%)
  between operations  0.64 us (1%)
    pallas_call x1, Pallas kernels, on_device(): pl.pallas_call(functools.partial(kernel, sizes), out_shape=(jax.ShapeDtyp...  55.1 us
    unnamed x2, local copies, waits for them, and re-layouts  1.41 us

profile of v2, /device:TPU:1, one launch (start us, length us, event | category | flops | bytes accessed | tf_op | source)
XLA Modules:
  0.0 57.1 jit_solution(13298914870607035226)
XLA Ops:
  0.6 55.1 %shard_map.86 = (f32[27,4,8,128]{3,2,1,0:T(8,128)S(1)}, f32[7,1,8,512]{3,2,1,0:T(8,128)S(1)}) custom-call(f32[27,4,8,128]{3,2,1,0:T(8,128)} %pop_in.1, f32[7,1,8,512]{3,2,1,0:T(8,128)} %th_in.1, f32[3,4,8,128]{3,2,1,0:T(8,128)} %vel_in.1, s32[4,8,128]{2,1,0:T(8,128)} %solid_in.1, s32[1,8,512]{2,1,0:T(8,128)} %ph_in.1, f32[4]{0:T(128)} %cond_in.1, f32[27]{0:T(128)} %rates_in.1), custom_call_target="tpu_custom_call" | custom-call | tf_op jit(solution)/shard_map/pallas_call | solution.py:495
  55.7 0.8 %copy.11 = f32[27,4,8,128]{3,2,1,0:T(8,128)} copy(f32[27,4,8,128]{3,2,1,0:T(8,128)S(1)} %get-tuple-element.4) | data formatting | bytes 884736
  56.5 0.6 %copy.12 = f32[7,1,8,512]{3,2,1,0:T(8,128)} copy(f32[7,1,8,512]{3,2,1,0:T(8,128)S(1)} %get-tuple-element.5) | data formatting | bytes 229376

commit v3 on v2

--- a/solution.py
+++ b/solution.py
@@ -15,7 +15,7 @@
 MESH = pl.DeviceIdType.MESH
 F32 = jnp.float32
 
-RING = [(-1, -1), (-1, 0), "x-", (-1, 1), (0, 1), "y+", (1, 1), (1, 0), "x+", (1, -1), (0, -1), "y-", (0, 0), "0", "z+", "z-"]
+RING = [(-1, -1), (-1, 0), (-1, 1), (0, 1), (1, 1), (1, 0), (1, -1), (0, -1), (0, 0), "0", "x+", "x-", "y+", "y-", "z+", "z-"]
 THERMAL = {"0": (0, 0, 0), "x+": (1, 0, 0), "x-": (-1, 0, 0), "y+": (0, 1, 0), "y-": (0, -1, 0), "z+": (0, 0, 1), "z-": (0, 0, -1)}
 HOME_ORDER = [0, 5, 6, 3, 4, 1, 2]
 HEAT_ORDER = ["0", "x+", "x-", "y+", "y-", "z+", "z-"]
@@ -32,9 +32,9 @@
             VELOCITY.append(entry + (c,))
 COUNT = len(VELOCITY)
 FLOW = [(a, b, c) for a in (-1, 0, 1) for b in (-1, 0, 1) for c in (-1, 0, 1)]
-X_GROUP = {1: (14, 24), -1: (0, 10)}
-Y_GROUP = {1: [(7, 17)], -1: [(21, 28), (0, 3)]}
-EDGE_GROUP = {(-1, -1): (0, 3), (-1, 1): (7, 10), (1, 1): (14, 17), (1, -1): (21, 24)}
+X_GROUP = {-1: (0, 9), 1: (12, 21)}
+Y_GROUP = {1: [(6, 15)], -1: [(18, 24), (0, 3)]}
+EDGE_GROUP = {(-1, -1): (0, 3), (-1, 1): (6, 9), (1, 1): (12, 15), (1, -1): (18, 21)}
 X_SLOT, XH_SLOT, H_SLOT = 0, 1, 6
 PLANES = 4
 ROW = 8
@@ -68,6 +68,15 @@
     s, t = SOURCE_ROW[b]
     for span in Y_GROUP[b]:
         MESSAGES.append(((0, 0, b), span, (2, 7), (2, 7), (s, s + 1), (t, t + 1)))
+
+FIRST_HEAT = len(MESSAGES)
+for a in (1, -1):
+    q = HEAT_AT[HEAT_ORDER.index("x+" if a == 1 else "x-")]
+    MESSAGES.append(((0, a, 0), (q, q + 1), (5, 7), (0, 2), (ROW, ROW + 8), (ROW, ROW + 8)))
+for b in (1, -1):
+    q = HEAT_AT[HEAT_ORDER.index("y+" if b == 1 else "y-")]
+    s, t = SOURCE_ROW[b]
+    MESSAGES.append(((0, 0, b), (q, q + 1), (2, 7), (2, 7), (s, s + 1), (t, t + 1)))
 
 RELAXED = [m for m in [(p, q, r) for p in range(3) for q in range(3) for r in range(3)] if m not in ((0, 0, 0), (0, 0, 1), (0, 1, 0), (1, 0, 0))]
 COEF = {}
@@ -206,18 +215,11 @@
                 both = jnp.where(lane < 64, ph_ref[0, :, right], ph_ref[0, :, left]).astype(F32)
             both = turn(both, 16 * k + 8)
             pack = both if pack is None else jnp.where(lane // 16 == k, both, pack)
-        aps[m] = pack
+        aps[m, 0] = pack
+        aps[m, 1] = sum_heat([th_ref[k, 0, :, 128 * m : 128 * m + 128] for k in range(7)])
     apr[mine] = aps[mine]
     ar[mine] = th_ref[:, 0, :, chunk(mine)]
     ari[mine] = ph_ref[0, :, chunk(mine)]
-    pl.semaphore_wait(barrier, len(others))
-    a_copies = []
-    for d in (2, 1, 3):
-        target = lax.rem(mine + d, 4)
-        to = device((d, 0, 0))
-        for n, (src, dst) in enumerate(((th_ref.at[:, 0, :, chunk(target)], ar.at[mine]), (ph_ref.at[0, :, chunk(target)], ari.at[mine]), (aps.at[target], apr.at[mine]))):
-            a_copies.append(pltpu.make_async_remote_copy(src_ref=src, dst_ref=dst, send_sem=a_send.at[n, d - 1], recv_sem=a_recv.at[n, d - 1], device_id=to, device_id_type=MESH))
-            a_copies[-1].start()
 
     group = [(unit == unit) & (((lane - center(p) + 16) % 128) < 32) for p in range(4)]
     for copy in loads[2:5]:
@@ -239,7 +241,6 @@
             tile = value if tile is None else jnp.where(group[p], value, tile)
         return tile
 
-    z_copies = []
     for n in range(8):
         low, high = None, None
         for k, field in enumerate(fields[4 * n : 4 * n + 4]):
@@ -248,10 +249,6 @@
             high = value if high is None else jnp.where(unit // 8 == (k + 1) % 4, value, high)
         zs[0, n] = low
         zs[1, n] = high
-        if n % 4 == 3:
-            for side, d in ((0, 1), (1, -1)):
-                z_copies.append(pltpu.make_async_remote_copy(src_ref=zs.at[side, n - 3 : n + 1], dst_ref=zr.at[side, n - 3 : n + 1], send_sem=z_send.at[side, n // 4], recv_sem=z_recv.at[side, n // 4], device_id=device((d, 0, 0)), device_id_type=MESH))
-                z_copies[-1].start()
 
     loads[5].wait()
     loads[6].wait()
@@ -265,8 +262,16 @@
     def coef(k, kind):
         return coefs[COEF[k, kind]]
 
-    for copy in a_copies:
-        copy.wait()
+    pl.semaphore_wait(barrier, len(others))
+    first_copies, late_copies = [], []
+    for d in (2, 1, 3):
+        target = lax.rem(mine + d, 4)
+        for n, (src, dst) in enumerate(((aps.at[target], apr.at[mine]), (th_ref.at[:, 0, :, chunk(target)], ar.at[mine]), (ph_ref.at[0, :, chunk(target)], ari.at[mine]))):
+            copy = pltpu.make_async_remote_copy(src_ref=src, dst_ref=dst, send_sem=a_send.at[n, d - 1], recv_sem=a_recv.at[n, d - 1], device_id=device((d, 0, 0)), device_id_type=MESH)
+            (late_copies if n else first_copies).append(copy)
+    z_copies = [pltpu.make_async_remote_copy(src_ref=zs.at[side], dst_ref=zr.at[side], send_sem=z_send.at[side], recv_sem=z_recv.at[side], device_id=device((d, 0, 0)), device_id_type=MESH) for side, d in ((0, 1), (1, -1))]
+    for copy in first_copies + z_copies:
+        copy.start()
 
     def omega_of(ids):
         level = jnp.full((8, 128), cond_ref[3], F32)
@@ -274,17 +279,15 @@
             level = jnp.where(ids == n, cond_ref[n], level)
         return 1.0 / (0.5 + 4.0 * level)
 
+    for copy in first_copies:
+        copy.wait()
     for p in range(4):
-        g = [turn(ar[p, k], center(p)) for k in range(7)]
-        for k in range(7):
-            stage[HEAT_AT[k], p] = g[k]
-        aux[0, p] = sum_heat(g)
-        aux[4, p] = omega_of(turn(ari[p], center(p)))
+        aux[0, p] = turn(apr[p, 1], center(p))
     tiles = []
     for k in range(8):
         tile = None
         for p in range(4):
-            value = turn(apr[p], center(p) - 16 * k - 8)
+            value = turn(apr[p, 0], center(p) - 16 * k - 8)
             tile = value if tile is None else jnp.where(group[p], value, tile)
         tiles.append(tile)
     for k in range(7):
@@ -315,13 +318,9 @@
     def own_slot(q, s):
         return H_SLOT if s == 4 else slot_of(VELOCITY[q][0], s)
 
-    def put(parity, s, flow, heat):
-        for key in FLOW:
-            q = FLOW_AT[key]
-            post[parity, q, own_slot(q, s), ROW : ROW + 8] = flow[key]
-        for k in range(7):
-            q = HEAT_AT[k]
-            post[parity, q, own_slot(q, s), ROW : ROW + 8] = heat[k]
+    def put(parity, s, tiles):
+        for q, value in tiles.items():
+            post[parity, q, own_slot(q, s), ROW : ROW + 8] = value
 
     def window(b):
         return slice(ROW - b, ROW - b + 8)
@@ -347,45 +346,80 @@
                 base = jnp.where(lane == spot, post[parity, q, slot_of(a, p - a), rows], base)
         return turn(base, amount)
 
-    def flow_arrivals(parity, s):
-        f = {}
-        for key in FLOW:
-            q = FLOW_AT[key]
-            if key == (0, 0, 0):
-                f[key] = post[parity, q, own_slot(q, s), ROW : ROW + 8]
-                continue
-            back = FLOW_AT[tuple(-v for v in key)]
-            value = arrive(parity, q, s)
-            f[key] = jnp.where(value != value, post[parity, back, own_slot(back, s), ROW : ROW + 8], value)
-        return f
-
-    def halo_rolls(parity, inner):
-        for q in range(COUNT):
+    def flow_arrival(parity, s, key):
+        q = FLOW_AT[key]
+        if key == (0, 0, 0):
+            return post[parity, q, own_slot(q, s), ROW : ROW + 8]
+        back = FLOW_AT[tuple(-v for v in key)]
+        value = arrive(parity, q, s)
+        return jnp.where(value != value, post[parity, back, own_slot(back, s), ROW : ROW + 8], value)
+
+    def needs_edge(s, key):
+        a, b, c = key
+        return a != 0 and b != 0 and (s == 4 or (s == 0 and a == 1) or (s == 3 and a == -1))
+
+    def halo_rolls(parity, kind):
+        for q in range(27):
             a, b, c = VELOCITY[q]
-            if c and inner:
+            if c and kind == "own":
                 hro[q] = turn(post[parity, q, H_SLOT, window(b)], 32 * a + c)
-            elif c and a:
+            elif c and a and kind == ("edge" if b else "face"):
                 hrx[q] = turn(post[parity, q, XH_SLOT, window(b)], 32 * a + c)
 
-    def start(parity, s, f, g, turned):
-        heat_sum = sum_heat(g)
+    def start_flow(parity, s, f, g, turned):
         old = aux[0, s]
-        heat = old if turned is None else jnp.where(turned, heat_sum, old)
+        heat = old if turned is None else jnp.where(turned, sum_heat(g), old)
         flow, (inverse, jx, jy, jz) = collide_flow(f, heat, coef)
-        speed = [aux[1 + n, s] for n in range(3)]
         if turned is not None:
             jz = jz + (0.5 * BUOYANCY) * (old - REFERENCE_HEAT)
             fresh = [j * inverse for j in (jx, jy, jz)]
             fresh = [jnp.where(v == v, v, 0.0) for v in fresh]
-            speed = [jnp.where(turned, fresh[n], speed[n]) for n in range(3)]
             aux[0, s] = heat
             for n in range(3):
-                aux[1 + n, s] = speed[n]
-        put(parity, s, flow, collide_heat(g, speed, aux[4, s]))
-
-    for s in (0, 3, 4, 1, 2):
-        start(0, s, {key: stage[FLOW_AT[key], s] for key in FLOW}, [stage[HEAT_AT[k], s] for k in range(7)], None)
-    for copy in round_copies(0):
+                aux[1 + n, s] = jnp.where(turned, fresh[n], aux[1 + n, s])
+        put(parity, s, {FLOW_AT[key]: flow[key] for key in FLOW})
+
+    def start_heat(parity, s, g):
+        out = collide_heat(g, [aux[1 + n, s] for n in range(3)], aux[4, s])
+        put(parity, s, {HEAT_AT[k]: out[k] for k in range(7)})
+
+    def staged(s, keys):
+        return {key: stage[FLOW_AT[key], s] for key in keys}
+
+    def staged_heat(s):
+        return [stage[HEAT_AT[k], s] for k in range(7)]
+
+    def heat_arrivals(parity):
+        for k in (5, 6):
+            q = HEAT_AT[k]
+            hro[q] = turn(post[parity, q, H_SLOT, ROW : ROW + 8], VELOCITY[q][2])
+        for s in range(5):
+            for k in range(7):
+                stage[HEAT_AT[k], s] = arrive(parity, HEAT_AT[k], s)
+
+    def heat_collide(parity):
+        for s in range(5):
+            start_heat(parity, s, staged_heat(s))
+
+    first = round_copies(0)
+    for s in (4, 0, 3):
+        start_flow(0, s, staged(s, FLOW), None, None)
+    for copy in first[:FIRST_X]:
+        copy.start()
+    for copy in late_copies:
+        copy.start()
+    for s in (1, 2):
+        start_flow(0, s, staged(s, FLOW), None, None)
+    for copy in first[FIRST_X:FIRST_HEAT]:
+        copy.start()
+    for copy in late_copies:
+        copy.wait()
+    for p in range(4):
+        for k in range(7):
+            stage[HEAT_AT[k], p] = turn(ar[p, k], center(p))
+        aux[4, p] = omega_of(turn(ari[p], center(p)))
+    heat_collide(0)
+    for copy in first[FIRST_HEAT:]:
         copy.start()
 
     total = STEPS * WINDOWS
@@ -438,41 +472,84 @@
         after = lax.rem(step, 2)
         turned = jnp.broadcast_to(step == STEPS, (8, 128))
         copies = round_copies(before)
-
-        def pair(s):
-            start(after, s, flow_arrivals(before, s), [arrive(before, HEAT_AT[k], s) for k in range(7)], turned)
-
-        for copy in copies[FIRST_Y:]:
+        later = round_copies(after)
+
+        def receive_heat():
+            for copy in copies[FIRST_HEAT:]:
+                copy.wait()
+            heat_arrivals(before)
+
+        def send_heat():
+            heat_collide(after)
+            for copy in later[FIRST_HEAT:]:
+                copy.start()
+
+        @pl.when(step == STEPS)
+        def _():
+            receive_heat()
+
+        @pl.when(step > STEPS)
+        def _():
+            receive_heat()
+
+            @pl.when(step < total - 1)
+            def _():
+                send_heat()
+
+            @pl.when(step == total - 1)
+            def _():
+                heat_collide(after)
+                home_start(after)
+
+        for copy in copies[FIRST_Y:FIRST_HEAT]:
             copy.wait()
-        halo_rolls(before, True)
-        pair(1)
-        pair(2)
-        for copy in copies[:FIRST_Y]:
+        halo_rolls(before, "own")
+        for s in (1, 2):
+            start_flow(after, s, {key: flow_arrival(before, s, key) for key in FLOW}, staged_heat(s), turned)
+        for copy in copies[FIRST_X:FIRST_Y]:
             copy.wait()
-        halo_rolls(before, False)
-        for s in (0, 3, 4):
-            pair(s)
-
-        @pl.when(step == total - 1)
+        halo_rolls(before, "face")
+        for s in (4, 0, 3):
+            for key in FLOW:
+                if not needs_edge(s, key):
+                    stage[FLOW_AT[key], s] = flow_arrival(before, s, key)
+        for copy in copies[:FIRST_X]:
+            copy.wait()
+        halo_rolls(before, "edge")
+        for s in (4, 0, 3):
+            f = {key: flow_arrival(before, s, key) if needs_edge(s, key) else stage[FLOW_AT[key], s] for key in FLOW}
+            start_flow(after, s, f, staged_heat(s), turned)
+            if s == 0:
+                for copy in later[:2]:
+                    copy.start()
+            if s == 3:
+                for copy in later[2:FIRST_X]:
+                    copy.start()
+        for copy in later[FIRST_X:FIRST_HEAT]:
+            copy.start()
+
+        @pl.when(step < STEPS)
         def _():
-            home_start(after)
-
-        for copy in round_copies(after):
-            copy.start()
+            receive_heat()
+            send_heat()
+
+        @pl.when(step == STEPS)
+        def _():
+            send_heat()
+
         return carry
 
     lax.fori_loop(1, total, advance, 0)
 
     last = (total - 1) % 2
-    copies = round_copies(last)
+    copies = round_copies(last)[:FIRST_HEAT]
     for copy in copies:
         copy.wait()
-    halo_rolls(last, True)
-    halo_rolls(last, False)
+    for kind in ("own", "face", "edge"):
+        halo_rolls(last, kind)
     for p in range(4):
-        f = flow_arrivals(last, p)
         for n, key in enumerate(FLOW):
-            fout[n, p] = jnp.where(solid_ref[p] != 0, pop_ref[n, p], turn(f[key], -center(p)))
+            fout[n, p] = jnp.where(solid_ref[p] != 0, pop_ref[n, p], turn(flow_arrival(last, p, key), -center(p)))
     perform(home_copies(), lambda copy: copy.wait())
     row = lax.broadcasted_iota(jnp.int32, (8, 128), 0)
     for n in range(4):
@@ -485,6 +562,14 @@
             tout[k, 0, :, 128 * n : 128 * n + 128] = tiles[k]
 
 
+def write_out(flow, heat, fout, tout, sem):
+    copies = [pltpu.make_async_copy(src, dst, sem.at[n]) for n, (src, dst) in enumerate(((flow, fout), (heat, tout)))]
+    for copy in copies:
+        copy.start()
+    for copy in copies:
+        copy.wait()
+
+
 def solution(mesh):
     sizes = dict(mesh.shape)
 
@@ -492,7 +577,7 @@
         vmem = pl.BlockSpec(memory_space=pltpu.VMEM)
         hbm = pl.BlockSpec(memory_space=pltpu.HBM)
         tile = (8, 128)
-        return pl.pallas_call(
+        flow, heat = pl.pallas_call(
             functools.partial(kernel, sizes),
             out_shape=(jax.ShapeDtypeStruct(populations.shape, F32), jax.ShapeDtypeStruct(thermal.shape, F32)),
             in_specs=[hbm] * 7,
@@ -508,8 +593,8 @@
                 pltpu.VMEM((COUNT,) + tile, F32),
                 pltpu.VMEM((4, 7) + tile, F32),
                 pltpu.VMEM((4,) + tile, jnp.int32),
-                pltpu.VMEM((4,) + tile, F32),
-                pltpu.VMEM((4,) + tile, F32),
+                pltpu.VMEM((4, 2) + tile, F32),
+                pltpu.VMEM((4, 2) + tile, F32),
                 pltpu.VMEM((2, 8) + tile, F32),
                 pltpu.VMEM((2, 8) + tile, F32),
                 pltpu.VMEM((4, 7) + tile, F32),
@@ -520,13 +605,22 @@
                 pltpu.SemaphoreType.DMA((2, len(MESSAGES))),
                 pltpu.SemaphoreType.DMA((3, 3)),
                 pltpu.SemaphoreType.DMA((3, 3)),
-                pltpu.SemaphoreType.DMA((2, 2)),
-                pltpu.SemaphoreType.DMA((2, 2)),
+                pltpu.SemaphoreType.DMA((2,)),
+                pltpu.SemaphoreType.DMA((2,)),
                 pltpu.SemaphoreType.DMA((5, 4)),
                 pltpu.SemaphoreType.DMA((5, 4)),
             ],
             compiler_params=pltpu.CompilerParams(collective_id=0, has_side_effects=True, vmem_limit_bytes=48 * 1024 * 1024),
         )(*[pltpu.with_memory_space_constraint(v, pltpu.HBM) for v in (populations, thermal, velocity_prev, solid, phase_ids, conductivity, rates)])
+        anywhere = pl.BlockSpec(memory_space=pl.ANY)
+        return pl.pallas_call(
+            write_out,
+            out_shape=(jax.ShapeDtypeStruct(flow.shape, F32), jax.ShapeDtypeStruct(heat.shape, F32)),
+            in_specs=[anywhere] * 2,
+            out_specs=(anywhere, anywhere),
+            scratch_shapes=[pltpu.SemaphoreType.DMA((2,))],
+            compiler_params=pltpu.CompilerParams(vmem_limit_bytes=4 * 1024 * 1024),
+        )(flow, heat)
 
     in_specs = (
         P(None, "gx", "gy", "grp"),

time: 57.6 us -> 55.8 us (0.969)
  local copies, waits for them, and re-layouts: 1.41 us -> 0 us
    unnamed x2 -> x0, local copies, waits for them, and re-layouts: 1.41 us -> none
    pallas_call x1, Pallas kernels: 55.1 us -> 54.3 us  [on_device(): pl.pallas_call(functools.partial(kernel, sizes), out_shape=(jax.ShapeDtyp...]
    pallas_call x0 -> x1, Pallas kernels: none -> 0.81 us  [on_device(): pl.pallas_call(write_out, out_shape=(jax.ShapeDtypeStruct(flow.shape, F32...]
where the time goes in v3:
time: 55.8 us; the launch traced here: 55.7 us
  Pallas kernels  55.1 us (99%)
  between operations  0.64 us (1%)
    pallas_call x1, Pallas kernels, on_device(): pl.pallas_call(functools.partial(kernel, sizes), out_shape=(jax.ShapeDtyp...  54.3 us

profile of v3, /device:TPU:1, one launch (start us, length us, event | category | flops | bytes accessed | tf_op | source)
XLA Modules:
  0.0 55.7 jit_solution(17124200514481543827)
XLA Ops:
  0.6 54.3 %shard_map.86 = (f32[27,4,8,128]{3,2,1,0:T(8,128)S(1)}, f32[7,1,8,512]{3,2,1,0:T(8,128)S(1)}) custom-call(f32[27,4,8,128]{3,2,1,0:T(8,128)} %pop_in.1, f32[7,1,8,512]{3,2,1,0:T(8,128)} %th_in.1, f32[3,4,8,128]{3,2,1,0:T(8,128)} %vel_in.1, s32[4,8,128]{2,1,0:T(8,128)} %solid_in.1, s32[1,8,512]{2,1,0:T(8,128)} %ph_in.1, f32[4]{0:T(128)} %cond_in.1, f32[27]{0:T(128)} %rates_in.1), custom_call_target="tpu_custom_call" | custom-call | tf_op jit(solution)/shard_map/pallas_call | solution.py:580
  54.9 0.8 %shard_map.87 = (f32[27,4,8,128]{3,2,1,0:T(8,128)}, f32[7,1,8,512]{3,2,1,0:T(8,128)}) custom-call(f32[27,4,8,128]{3,2,1,0:T(8,128)S(1)} %get-tuple-element.4.flow, f32[7,1,8,512]{3,2,1,0:T(8,128)S(1)} %get-tuple-element.5.heat), custom_call_target="tpu_custom_call" | custom-call | tf_op jit(solution)/shard_map/pallas_call | solution.py:616

commit v4 on v3

--- a/solution.py
+++ b/solution.py
@@ -402,10 +402,10 @@
             start_heat(parity, s, staged_heat(s))
 
     first = round_copies(0)
-    for s in (4, 0, 3):
+    for s in (4, 3, 0):
         start_flow(0, s, staged(s, FLOW), None, None)
-    for copy in first[:FIRST_X]:
-        copy.start()
+        for copy in first[:2] if s == 0 else first[2:FIRST_X] if s == 3 else []:
+            copy.start()
     for copy in late_copies:
         copy.start()
     for s in (1, 2):
@@ -516,16 +516,16 @@
         for copy in copies[:FIRST_X]:
             copy.wait()
         halo_rolls(before, "edge")
-        for s in (4, 0, 3):
+        for s in (4, 3, 0):
             f = {key: flow_arrival(before, s, key) if needs_edge(s, key) else stage[FLOW_AT[key], s] for key in FLOW}
             start_flow(after, s, f, staged_heat(s), turned)
             if s == 0:
-                for copy in later[:2]:
+                for copy in later[:2] + later[FIRST_X + 1 : FIRST_Y]:
                     copy.start()
             if s == 3:
-                for copy in later[2:FIRST_X]:
+                for copy in later[2:FIRST_X] + later[FIRST_X : FIRST_X + 1]:
                     copy.start()
-        for copy in later[FIRST_X:FIRST_HEAT]:
+        for copy in later[FIRST_Y:FIRST_HEAT]:
             copy.start()
 
         @pl.when(step < STEPS)
@@ -542,14 +542,28 @@
     lax.fori_loop(1, total, advance, 0)
 
     last = (total - 1) % 2
-    copies = round_copies(last)[:FIRST_HEAT]
-    for copy in copies:
-        copy.wait()
-    for kind in ("own", "face", "edge"):
-        halo_rolls(last, kind)
-    for p in range(4):
+    copies = round_copies(last)
+
+    def finish(p, edge):
         for n, key in enumerate(FLOW):
-            fout[n, p] = jnp.where(solid_ref[p] != 0, pop_ref[n, p], turn(flow_arrival(last, p, key), -center(p)))
+            if needs_edge(p, key) == edge:
+                fout[n, p] = jnp.where(solid_ref[p] != 0, pop_ref[n, p], turn(flow_arrival(last, p, key), -center(p)))
+
+    for copy in copies[FIRST_Y:FIRST_HEAT]:
+        copy.wait()
+    halo_rolls(last, "own")
+    for p in (1, 2):
+        finish(p, False)
+    for copy in copies[FIRST_X:FIRST_Y]:
+        copy.wait()
+    halo_rolls(last, "face")
+    for p in (0, 3):
+        finish(p, False)
+    for copy in copies[:FIRST_X]:
+        copy.wait()
+    halo_rolls(last, "edge")
+    for p in (0, 3):
+        finish(p, True)
     perform(home_copies(), lambda copy: copy.wait())
     row = lax.broadcasted_iota(jnp.int32, (8, 128), 0)
     for n in range(4):

time: 55.8 us -> 55 us (0.986)
  Pallas kernels: 55.1 us -> 54.2 us
    pallas_call x1, Pallas kernels: 54.3 us -> 53.4 us  [on_device(): pl.pallas_call(functools.partial(kernel, sizes), out_shape=(jax.ShapeDtyp...]
where the time goes in v4:
time: 55 us; the launch traced here: 54.8 us
  Pallas kernels  54.2 us (99%)
  between operations  0.64 us (1%)
    pallas_call x1, Pallas kernels, on_device(): pl.pallas_call(functools.partial(kernel, sizes), out_shape=(jax.ShapeDtyp...  53.4 us

profile of v4, /device:TPU:1, one launch (start us, length us, event | category | flops | bytes accessed | tf_op | source)
XLA Modules:
  0.0 54.8 jit_solution(14376099938687770657)
XLA Ops:
  0.6 53.4 %shard_map.86 = (f32[27,4,8,128]{3,2,1,0:T(8,128)S(1)}, f32[7,1,8,512]{3,2,1,0:T(8,128)S(1)}) custom-call(f32[27,4,8,128]{3,2,1,0:T(8,128)} %pop_in.1, f32[7,1,8,512]{3,2,1,0:T(8,128)} %th_in.1, f32[3,4,8,128]{3,2,1,0:T(8,128)} %vel_in.1, s32[4,8,128]{2,1,0:T(8,128)} %solid_in.1, s32[1,8,512]{2,1,0:T(8,128)} %ph_in.1, f32[4]{0:T(128)} %cond_in.1, f32[27]{0:T(128)} %rates_in.1), custom_call_target="tpu_custom_call" | custom-call | tf_op jit(solution)/shard_map/pallas_call | solution.py:594
  54.0 0.8 %shard_map.87 = (f32[27,4,8,128]{3,2,1,0:T(8,128)}, f32[7,1,8,512]{3,2,1,0:T(8,128)}) custom-call(f32[27,4,8,128]{3,2,1,0:T(8,128)S(1)} %get-tuple-element.4.flow, f32[7,1,8,512]{3,2,1,0:T(8,128)S(1)} %get-tuple-element.5.heat), custom_call_target="tpu_custom_call" | custom-call | tf_op jit(solution)/shard_map/pallas_call | solution.py:630

commit v5 on v4

--- a/solution.py
+++ b/solution.py
@@ -361,7 +361,7 @@
     def halo_rolls(parity, kind):
         for q in range(27):
             a, b, c = VELOCITY[q]
-            if c and kind == "own":
+            if c and kind == ("own" if b else "still"):
                 hro[q] = turn(post[parity, q, H_SLOT, window(b)], 32 * a + c)
             elif c and a and kind == ("edge" if b else "face"):
                 hrx[q] = turn(post[parity, q, XH_SLOT, window(b)], 32 * a + c)
@@ -501,11 +501,17 @@
                 heat_collide(after)
                 home_start(after)
 
+        halo_rolls(before, "still")
+        for s in (1, 2):
+            for key in FLOW:
+                if key[1] == 0:
+                    stage[FLOW_AT[key], s] = flow_arrival(before, s, key)
         for copy in copies[FIRST_Y:FIRST_HEAT]:
             copy.wait()
         halo_rolls(before, "own")
         for s in (1, 2):
-            start_flow(after, s, {key: flow_arrival(before, s, key) for key in FLOW}, staged_heat(s), turned)
+            f = {key: flow_arrival(before, s, key) if key[1] else stage[FLOW_AT[key], s] for key in FLOW}
+            start_flow(after, s, f, staged_heat(s), turned)
         for copy in copies[FIRST_X:FIRST_Y]:
             copy.wait()
         halo_rolls(before, "face")
@@ -551,6 +557,7 @@
 
     for copy in copies[FIRST_Y:FIRST_HEAT]:
         copy.wait()
+    halo_rolls(last, "still")
     halo_rolls(last, "own")
     for p in (1, 2):
         finish(p, False)

time: 55 us -> 55.2 us (level)
  no operation moved by 1% of the time
where the time goes in v5:
time: 55.2 us; the launch traced here: 55 us
  Pallas kernels  54.3 us (98%)
  between operations  0.64 us (1%)
    pallas_call x1, Pallas kernels, on_device(): pl.pallas_call(functools.partial(kernel, sizes), out_shape=(jax.ShapeDtyp...  53.5 us

profile of v5, /device:TPU:1, one launch (start us, length us, event | category | flops | bytes accessed | tf_op | source)
XLA Modules:
  0.0 55.0 jit_solution(7841575237449107827)
XLA Ops:
  0.6 53.5 %shard_map.86 = (f32[27,4,8,128]{3,2,1,0:T(8,128)S(1)}, f32[7,1,8,512]{3,2,1,0:T(8,128)S(1)}) custom-call(f32[27,4,8,128]{3,2,1,0:T(8,128)} %pop_in.1, f32[7,1,8,512]{3,2,1,0:T(8,128)} %th_in.1, f32[3,4,8,128]{3,2,1,0:T(8,128)} %vel_in.1, s32[4,8,128]{2,1,0:T(8,128)} %solid_in.1, s32[1,8,512]{2,1,0:T(8,128)} %ph_in.1, f32[4]{0:T(128)} %cond_in.1, f32[27]{0:T(128)} %rates_in.1), custom_call_target="tpu_custom_call" | custom-call | tf_op jit(solution)/shard_map/pallas_call | solution.py:601
  54.2 0.8 %shard_map.87 = (f32[27,4,8,128]{3,2,1,0:T(8,128)}, f32[7,1,8,512]{3,2,1,0:T(8,128)}) custom-call(f32[27,4,8,128]{3,2,1,0:T(8,128)S(1)} %get-tuple-element.4.flow, f32[7,1,8,512]{3,2,1,0:T(8,128)S(1)} %get-tuple-element.5.heat), custom_call_target="tpu_custom_call" | custom-call | tf_op jit(solution)/shard_map/pallas_call | solution.py:637
